TPU v7x, 32 devices: a whole 2x2x4 slice. The times are simulated.
32 devices in a mesh: seq: 8 (over z, y), tp: 4 (over x, core).
Axes of the slice: x: 2, y: 2, z: 4, core: 2. Of those that a mesh axis runs over, the one named last changes fastest.
Arguments:
- tokens: bfloat16 [4, 2048, 1024], P('tp', 'seq'), may hold values from -6 to 6
- lengths: int32 [4], replicated, may hold values from 256 to 2048, as said below
- forget: float32 [8], replicated, as said below
- w_mix: bfloat16 [1024, 4096], replicated, may hold values from -0.1875 to 0.1875
- w_out: bfloat16 [1024, 1024], replicated, may hold values from -0.1875 to 0.1875
- w_gate: bfloat16 [1024, 2816], P(None, 'tp'), may hold values from -0.1875 to 0.1875
- w_up: bfloat16 [1024, 2816], P(None, 'tp'), may hold values from -0.1875 to 0.1875
- w_down: bfloat16 [1024, 2816], P(None, 'tp'), may hold values from -0.109375 to 0.109375
- cotangent: bfloat16 [4, 2048, 1024], P('tp', 'seq'), may hold values from -6 to 6
Outputs:
- out: bfloat16 [4, 2048, 1024], P('tp', 'seq')
- d_tokens: bfloat16 [4, 2048, 1024], P('tp', 'seq')
- d_mix: float32 [1024, 4096], P('seq')
- d_out: float32 [1024, 1024], P('seq')
- d_gate: float32 [1024, 2816], P('seq', 'tp')
- d_up: float32 [1024, 2816], P('seq', 'tp')
- d_down: float32 [1024, 2816], P('seq', 'tp')
Inputs may be any that keep to these rules, and one draw needn't show every extreme that they name: Positions at and after lengths[i] of sequence i are padding; in every draw one sequence has all 2048 positions. A head's state is multiplied by exp(-forget) for every position that it moves on.
All inputs are finite; a program needn't handle non-finite values.
Results may differ from a plain program's by a relative error of at most 0.02.
Values may be sent and summed in bfloat16 or wider, within the bound.
No kernel may reach another device: no remote copies, remote signals or barrier semaphores. Data moves between devices by JAX's collectives and lax.ppermute only.
A program may use at most 384 MiB of HBM per device.

v0:
```python
from functools import partial
import math

import jax
import jax.numpy as jnp
import numpy as np
from jax import lax
from jax.experimental import pallas as pl
from jax.experimental.pallas import tpu as pltpu
from jax.sharding import PartitionSpec as P

HEADS = 8
HEAD = 128
HALF = HEADS // 2
PAIR = 2 * HEAD
EPSILON = 1e-06
BF = jnp.bfloat16
F32 = jnp.float32
SMALL = pl.BlockSpec(memory_space=pltpu.SMEM)
WHOLE = pl.BlockSpec(memory_space=pltpu.VMEM)
MIB = 1024 * 1024
ROOM = 4
BRIEF = 0.02
LONG = 6.0


def norm_scale(value):
    return lax.rsqrt(jnp.mean(value * value, axis=-1, keepdims=True) + EPSILON)


def norm_back(value, upstream):
    r = norm_scale(value)
    return r * upstream - value * (r * r * r * jnp.mean(value * upstream, axis=-1, keepdims=True))


def dot_nn(left, right):
    return jnp.dot(left, right, preferred_element_type=F32)


def dot_nt(left, right):
    return lax.dot_general(left, right, (((1,), (1,)), ((), ())), preferred_element_type=F32)


def dot_tn(left, right):
    return lax.dot_general(left, right, (((0,), (0,)), ((), ())), preferred_element_type=F32)


def rotation(places, width):
    table = np.floor(
        65536.0 / (2.0 * math.pi) * 10000.0 ** (-np.arange(width) / width) + 0.5
    ).astype(np.int32)
    phase = jnp.remainder(places[:, None] * jnp.asarray(table)[None, :], 65536)
    angle = phase.astype(F32) * (2.0 * math.pi / 65536.0)
    return (jnp.cos(angle), jnp.sin(angle))


def swap(array, axis, bit):
    count = lax.axis_size(axis)
    return lax.ppermute(array, axis, [(i, i ^ bit) for i in range(count)])


def tie(array, *others):
    return lax.optimization_barrier((array, *others))[0]


def positions(rows, columns):
    return lax.broadcasted_iota(jnp.int32, (rows, columns), 0).astype(F32)


def decay_grid(rate, span):
    gap = positions(span, span) - lax.broadcasted_iota(jnp.int32, (span, span), 1).astype(F32)
    return jnp.where(gap >= 0, jnp.exp(-rate * jnp.maximum(gap, 0.0)), 0.0)


def spread(values, cosine, sine):
    return jnp.concatenate([values * cosine, values * sine], axis=1).astype(BF)


def fold(grad, cosine, sine):
    return grad[:, :HEAD] * cosine + grad[:, HEAD:] * sine


def slope_of(raw):
    gate = jax.nn.sigmoid(raw)
    return gate * (1.0 + raw * (1.0 - gate))


def shape_of(shape, kind):
    return jax.ShapeDtypeStruct(shape, kind)


def params(room):
    return pltpu.CompilerParams(vmem_limit_bytes=int(room))


def cost(span_us):
    return pl.CostEstimate(flops=int(span_us * 1.1e9), bytes_accessed=1024, transcendentals=0)


class Line:
    def __init__(self):
        self.last = None
        self.more = []

    def wait(self, *arrays):
        self.more += arrays

    def hold(self, array):
        return array if self.last is None else tie(array, self.last)

    def swap(self, array, axis, bit):
        return swap(self.hold(array), axis, bit)

    def run(self, name, kernel, outs, scalars, arrays, time=BRIEF):
        arrays = list(arrays)
        arrays[0] = self.hold(arrays[0])
        if self.more:
            arrays[0] = tie(arrays[0], *self.more)
            self.more = []
        moved = sum(a.size * a.dtype.itemsize for a in arrays)
        moved += sum(math.prod(s) * jnp.dtype(k).itemsize for s, k in outs)
        results = pl.pallas_call(
            kernel,
            name=name,
            out_shape=[shape_of(s, k) for s, k in outs],
            in_specs=[SMALL] * len(scalars) + [WHOLE] * len(arrays),
            out_specs=[WHOLE] * len(outs),
            compiler_params=params(moved * 1.125 + ROOM * MIB),
            cost_estimate=cost(time),
        )(*scalars, *arrays)
        self.last = results[0]
        return results


def left_of(numbers, lengths, span):
    return lengths[numbers[2]] - (2 * numbers[1] + numbers[0]) * span


def valid_rows(numbers, lengths, shape):
    return lax.broadcasted_iota(jnp.int32, shape, 0) < left_of(numbers, lengths, shape[0])


def columns_of(w_mix, block, j):
    groups = w_mix.shape[1] // (4 * PAIR)
    return w_mix[:, (block * groups + j) * PAIR : (block * groups + j + 1) * PAIR]


def key_value_kernel(numbers, forget, tokens, cosine, sine, w_mix, normed, raw_key, key, value, send, keep):
    span, width = tokens.shape
    groups = width // PAIR
    inputs = tokens[...].astype(F32)
    rows = (inputs * norm_scale(inputs)).astype(BF)
    normed[...] = rows
    place = positions(span, HEAD)
    states = []
    for g in range(groups):
        lanes = slice(g * PAIR, (g + 1) * PAIR)
        raw = dot_nn(rows, columns_of(w_mix, 1, g))
        raw_key[:, lanes] = raw
        low = dot_nn(rows, columns_of(w_mix, 2, g)).astype(BF)
        value[:, lanes] = low
        active = raw * jax.nn.sigmoid(raw)
        for h in range(2):
            part = slice(h * HEAD, (h + 1) * HEAD)
            turned = spread(active[:, part], cosine[...], sine[...])
            start = 2 * (2 * g + h) * HEAD
            key[:, start : start + 2 * HEAD] = turned
            tail = jnp.exp(-forget[2 * g + h] * (span - 1.0 - place))
            states.append(dot_tn(turned, (low[:, part].astype(F32) * tail).astype(BF)).astype(BF))
    low_side = numbers[0] == 0
    for h in range(HALF):
        keep[h] = jnp.where(low_side, states[h], states[h + HALF])
        send[h] = jnp.where(low_side, states[h + HALF], states[h])


def query_kernel(
    numbers, lengths, forget, normed, key, value, cosine, sine, w_mix, cotangent,
    raw_query, query, update, scores, intra, down_low,
):
    span, width = normed.shape
    upstream = cotangent[...]
    down_low[...] = jnp.where(valid_rows(numbers, lengths, upstream.shape), upstream, jnp.zeros_like(upstream))
    groups = width // PAIR
    rows = normed[...]
    for g in range(groups):
        lanes = slice(g * PAIR, (g + 1) * PAIR)
        raw = dot_nn(rows, columns_of(w_mix, 0, g))
        raw_query[:, lanes] = raw
        update[:, lanes] = dot_nn(rows, columns_of(w_mix, 3, g))
        active = raw * jax.nn.sigmoid(raw)
        for h in range(2):
            head = 2 * g + h
            part = slice(head * HEAD, (head + 1) * HEAD)
            wide = slice(2 * head * HEAD, 2 * (head + 1) * HEAD)
            turned = spread(active[:, h * HEAD : (h + 1) * HEAD], cosine[...], sine[...])
            query[:, wide] = turned
            low = (dot_nt(turned, key[:, wide]) * decay_grid(forget[head], span)).astype(BF)
            scores[head] = low
            intra[:, part] = dot_nn(low, value[:, part])


def stand(numbers, backward):
    side, layer = numbers[0], numbers[1]
    low = side == 1 if backward else side == 0
    depth = 3 - layer if backward else layer
    return side, low, lax.rem(depth, 2) == 0, depth < 2


def block_rate(forget, side, h, span):
    return jnp.exp(jnp.zeros((1, HEAD), F32) - forget[side * HALF + h] * span)


def pair_kernel(backward, span, numbers, forget, keep, other, pair):
    side, low, _, _ = stand(numbers, backward)
    for h in range(HALF):
        rate = block_rate(forget, side, h, span)
        mine, theirs = keep[h].astype(F32), other[h].astype(F32)
        pair[h] = (jnp.where(low, rate, 1.0) * mine + jnp.where(low, 1.0, rate) * theirs).astype(BF)


def quad_kernel(backward, span, numbers, forget, pair, near, quad):
    side, _, even, _ = stand(numbers, backward)
    for h in range(HALF):
        rate = block_rate(forget, side, h, 2.0 * span)
        mine, theirs = pair[h].astype(F32), near[h].astype(F32)
        quad[h] = (jnp.where(even, rate, 1.0) * mine + jnp.where(even, 1.0, rate) * theirs).astype(BF)


def enter_kernel(backward, span, numbers, forget, near, far, keep, other, theirs, mine):
    side, low, even, early = stand(numbers, backward)
    for h in range(HALF):
        rate = block_rate(forget, side, h, span)
        double = block_rate(forget, side, h, 2.0 * span)
        from_near = jnp.where(even, 0.0, 1.0)
        from_far = jnp.where(early, 0.0, jnp.where(even, 1.0, double))
        before = from_near * near[h].astype(F32) + from_far * far[h].astype(F32)
        added = before * rate + jnp.where(low, keep[h].astype(F32), other[h].astype(F32))
        theirs[h] = jnp.where(low, added, before).astype(BF)
        mine[h] = jnp.where(low, before, added).astype(BF)


def scan_states(line, send, keep, numbers, forget, span, backward, fillers):
    name = "back" if backward else "fore"
    state = [(keep.shape, BF)]
    other = swap(send, "seq", 1)
    fillers[0](None)
    pair = line.run(name + "_pair", partial(pair_kernel, backward, span), state, [numbers, forget], [keep, other])[0]
    near = swap(pair, "seq", 2)
    fillers[1](other)
    quad = line.run(name + "_quad", partial(quad_kernel, backward, span), state, [numbers, forget], [pair, near])[0]
    far = swap(quad, "seq", 4)
    fillers[2](near)
    theirs, mine = line.run(
        name + "_enter", partial(enter_kernel, backward, span), state * 2, [numbers, forget], [near, far, keep, other]
    )
    theirs = swap(theirs, "seq", 1)
    fillers[3](far)
    return mine, theirs


def scan_any(state, forget, span, backward):
    count = lax.axis_size("seq")
    place = lax.axis_index("seq")
    ahead = count - 1 - place if backward else place
    carried = jnp.exp(-forget * span)[:, None, None]
    gathered = lax.all_gather(state, "seq")

    def one(hop, total):
        source = count - 1 - hop if backward else hop
        return total * carried + lax.dynamic_index_in_dim(gathered, source, 0, False).astype(F32)

    return lax.fori_loop(0, ahead, one, jnp.zeros(state.shape, F32)).astype(BF)


def by_side(side, mine, theirs):
    low = side == 0
    return jnp.where(low, jnp.concatenate([mine, theirs]), jnp.concatenate([theirs, mine]))


def scan(line, send, keep, numbers, forget, span, backward, fillers):
    if lax.axis_size("seq") == 8:
        return scan_states(line, send, keep, numbers, forget, span, backward, fillers)
    for filler in fillers:
        filler(None)
    whole = scan_any(by_side(numbers[0], keep, send), forget, span, backward)
    upper = numbers[0] == 0
    return jnp.where(upper, whole[:HALF], whole[HALF:]), jnp.where(upper, whole[HALF:], whole[:HALF])


def state_of(numbers, mine, theirs, h):
    first, second = (mine, theirs) if h < HALF else (theirs, mine)
    return jnp.where(numbers[0] == 0, first[h % HALF], second[h % HALF])


def mix_kernel(numbers, forget, theirs, mine, query, intra, update, tokens, w_out, attention, gated, resid, ffn_in):
    span, width = tokens.shape
    place = positions(span, HEAD)
    for h in range(HEADS):
        lanes = slice(h * HEAD, (h + 1) * HEAD)
        wide = slice(2 * h * HEAD, 2 * (h + 1) * HEAD)
        lead = jnp.exp(-forget[h] * (place + 1.0))
        attention[:, lanes] = intra[:, lanes] + dot_nn(query[:, wide], state_of(numbers, mine, theirs, h)) * lead
    whole = attention[...]
    low = (whole * norm_scale(whole) * update[...]).astype(BF)
    gated[...] = low
    after = tokens[...].astype(F32) + dot_nn(low, w_out[...])
    resid[...] = after
    ffn_in[...] = (after * norm_scale(after)).astype(BF)


def ffn_kernel(rows_0, rows_1, hidden_grad, w_gate, w_up, hidden, gate_grad, up_grad, back_0, back_1):
    span = rows_0.shape[0]
    for i, (rows, back) in enumerate(((rows_0, back_0), (rows_1, back_1))):
        block = slice(i * span, (i + 1) * span)
        gate_pre = dot_nt(rows[...], w_gate[...])
        up_pre = dot_nt(rows[...], w_up[...])
        hidden[block] = (gate_pre * up_pre).astype(BF)
        upstream = hidden_grad[block]
        gate_low = (upstream * up_pre).astype(BF)
        up_low = (upstream * gate_pre).astype(BF)
        gate_grad[block] = gate_low
        up_grad[block] = up_low
        back[...] = (dot_nn(gate_low, w_gate[...]) + dot_nn(up_low, w_up[...])).astype(BF)


def hidden_grad_kernel(rows_0, rows_1, rows_2, rows_3, w_down, near, far):
    span = rows_0.shape[0]
    for rows, target, block in (
        (rows_0, near, slice(0, span)),
        (rows_1, near, slice(span, 2 * span)),
        (rows_2, far, slice(0, span)),
        (rows_3, far, slice(span, 2 * span)),
    ):
        target[block] = dot_nt(rows[...], w_down[...])


def down_kernel(hidden_near, hidden_far, w_down, own, other, far, cross):
    span = own.shape[0]
    for source, target, block in (
        (hidden_near, own, slice(0, span)),
        (hidden_near, other, slice(span, 2 * span)),
        (hidden_far, far, slice(0, span)),
        (hidden_far, cross, slice(span, 2 * span)),
    ):
        target[...] = dot_nn(source[block], w_down[...]).astype(BF)


def add_kernel(first, second, total):
    total[...] = (first[...].astype(F32) + second[...].astype(F32)).astype(BF)


def out_kernel(numbers, lengths, part_0, part_1, part_2, resid, out):
    valid = valid_rows(numbers, lengths, resid.shape)
    down = part_0[...].astype(F32) + part_1[...].astype(F32) + part_2[...].astype(F32)
    out[...] = jnp.where(valid, resid[...] + down, 0.0).astype(BF)


def resid_kernel(
    forget, numbers, part_0, part_1, part_2, resid, down_low, attention, update, query, w_out,
    resid_grad, mix_grad, update_grad, attention_grad, send, keep,
):
    span, width = resid.shape
    ffn_grad = part_0[...].astype(F32) + part_1[...].astype(F32) + part_2[...].astype(F32)
    total = down_low[...].astype(F32) + norm_back(resid[...], ffn_grad)
    resid_grad[...] = total
    low = total.astype(BF)
    mix_grad[...] = low
    gated_grad = dot_nt(low, w_out[...])
    whole = attention[...]
    r = norm_scale(whole)
    update_grad[...] = (gated_grad * (whole * r)).astype(BF)
    upstream = gated_grad * update[...]
    back = r * upstream - whole * (r * r * r * jnp.mean(whole * upstream, axis=-1, keepdims=True))
    attention_grad[...] = back.astype(BF)
    place = positions(span, HEAD)
    moments = []
    for h in range(HEADS):
        lanes = slice(h * HEAD, (h + 1) * HEAD)
        wide = slice(2 * h * HEAD, 2 * (h + 1) * HEAD)
        first = jnp.exp(-forget[h] * place)
        moments.append(dot_tn(query[:, wide], (attention_grad[:, lanes].astype(F32) * first).astype(BF)).astype(BF))
    low_side = numbers[0] == 0
    for h in range(HALF):
        keep[h] = jnp.where(low_side, moments[h], moments[h + HALF])
        send[h] = jnp.where(low_side, moments[h + HALF], moments[h])


def early_kernel(
    numbers, forget, grad, value, key, query, scores, theirs, mine, raw_query, cosine, sine, update_grad, mix_grad,
    piece_0, piece_1, piece_2, piece_3, key_part, value_part, pieces,
):
    span, width = update_grad.shape
    place = positions(span, 2 * HEAD)
    for h in range(HEADS):
        lanes = slice(h * HEAD, (h + 1) * HEAD)
        wide = slice(2 * h * HEAD, 2 * (h + 1) * HEAD)
        upstream = grad[:, lanes]
        low = (dot_nt(upstream, value[:, lanes]) * decay_grid(forget[h], span)).astype(BF)
        lead = jnp.exp(-forget[h] * (place + 1.0))
        query_grad = dot_nn(low, key[:, wide]) + dot_nt(upstream, state_of(numbers, mine, theirs, h)) * lead
        slope = slope_of(raw_query[:, lanes])
        start = (h % 2) * HEAD
        pieces[h // 2, :, start : start + HEAD] = (slope * fold(query_grad, cosine[...], sine[...])).astype(BF)
        key_part[:, lanes] = fold(dot_tn(low, query[:, wide]), cosine[...], sine[...])
        value_part[:, lanes] = dot_tn(scores[h], upstream)
    for j in range(width // PAIR):
        columns = slice(j * PAIR, (j + 1) * PAIR)
        pieces[j, :, PAIR : 2 * PAIR] = update_grad[:, columns]
        pieces[j, :, 2 * PAIR :] = mix_grad[:, columns]
    for k, piece in enumerate((piece_0, piece_1, piece_2, piece_3)):
        piece[...] = pieces[numbers[2] ^ k]


def late_kernel(
    numbers, forget, theirs, mine, value, key, raw_key, cosine, sine, key_part, value_part,
    piece_0, piece_1, piece_2, piece_3, pieces,
):
    span, width = value.shape
    place = positions(span, HEAD)
    for h in range(HEADS):
        lanes = slice(h * HEAD, (h + 1) * HEAD)
        wide = slice(2 * h * HEAD, 2 * (h + 1) * HEAD)
        after = state_of(numbers, mine, theirs, h)
        rear = jnp.exp(-forget[h] * (span - place))
        key_grad = fold(dot_nt(value[:, lanes], after), cosine[...], sine[...]) * rear + key_part[:, lanes]
        value_grad = dot_nn(key[:, wide], after) * rear + value_part[:, lanes]
        start = (h % 2) * HEAD
        pieces[h // 2, :, start : start + HEAD] = (slope_of(raw_key[:, lanes]) * key_grad).astype(BF)
        pieces[h // 2, :, PAIR + start : PAIR + start + HEAD] = value_grad.astype(BF)
    for k, piece in enumerate((piece_0, piece_1, piece_2, piece_3)):
        piece[...] = pieces[numbers[2] ^ k]


BITS = {"y": 1, "z1": 2, "z2": 4}


def bit_of(numbers, name):
    return numbers[0] if name == "y" else numbers[1] % 2 if name == "z1" else numbers[1] // 2


def split_blocks(order, numbers, keep, send, parts, index):
    mine = bit_of(numbers, order[0]) == 0
    for place in range(4):
        rest = BITS[order[1]] * (place // 2) + BITS[order[2]] * (place % 2)
        zero, one = parts[rest], parts[rest + BITS[order[0]]]
        keep[(place, *index)] = jnp.where(mine, zero, one)
        send[(place, *index)] = jnp.where(mine, one, zero)


def mix_weight_kernel(groups, order, numbers, *refs):
    inputs, send, keep = refs[:-2], refs[-2], refs[-1]
    part = keep.shape[1]
    start = 0
    for left, right, low, high in groups:
        total = None
        for a, b in zip(left, right):
            term = dot_tn(inputs[a][...], inputs[b][:, low:high])
            total = term if total is None else total + term
        parts = [total[m * part : (m + 1) * part].astype(BF) for m in range(8)]
        split_blocks(order, numbers, keep, send, parts, (slice(None), slice(start, start + high - low)))
        start += high - low


def ffn_weight_kernel(order, numbers, *refs):
    near, far, rows, send, keep = refs[0], refs[1], refs[2:6], refs[-2], refs[-1]
    span = rows[0].shape[0]
    units = near.shape[1]
    part = keep.shape[2]
    step = 256
    for low in range(0, units, step):
        high = min(low + step, units)
        total = None
        for i in range(4):
            source = near if i < 2 else far
            term = dot_tn(source[(i % 2) * span : (i % 2 + 1) * span, low:high], rows[i][...])
            total = term if total is None else total + term
        parts = [total[:, m * part : (m + 1) * part].astype(BF) for m in range(8)]
        split_blocks(order, numbers, keep, send, parts, (slice(low, high), slice(None)))


def whole_mix_weight_kernel(groups, numbers, *refs):
    inputs, target = refs[:-1], refs[-1]
    start = 0
    for left, right, low, high in groups:
        total = None
        for a, b in zip(left, right):
            term = dot_tn(inputs[a][...], inputs[b][:, low:high])
            total = term if total is None else total + term
        target[:, start : start + high - low] = total.astype(BF)
        start += high - low


def whole_ffn_weight_kernel(numbers, *refs):
    near, far, rows, target = refs[0], refs[1], refs[2:6], refs[-1]
    span = rows[0].shape[0]
    total = None
    for i in range(4):
        source = near if i < 2 else far
        term = dot_tn(source[(i % 2) * span : (i % 2 + 1) * span], rows[i][...])
        total = term if total is None else total + term
    target[...] = total.astype(BF)


def join_kernel(name, numbers, other, keep, send, own):
    mine = bit_of(numbers, name)
    count = own.shape[0]
    for i in range(count):
        for target, half in ((own, mine), (send, 1 - mine)):
            total = keep[half * count + i].astype(F32) + other[half * count + i].astype(F32)
            target[i] = total.astype(target.dtype)


def sum_kernel(other, keep, total):
    total[...] = (keep[0].astype(F32) + other[0].astype(F32)).astype(total.dtype)


class Reduction:
    def __init__(self, line, name, numbers, order, blocks_first, kernel, whole_kernel, shape, arrays, time):
        self.line, self.name, self.numbers, self.order = line, name, numbers, order
        self.fast = lax.axis_size("seq") == 8
        self.blocks_first = blocks_first
        if self.fast:
            rows, columns = shape
            block = (rows // 8, columns) if blocks_first else (rows, columns // 8)
            outs = [((4, *block), BF)] * 2
            self.send, self.keep = line.run(name, partial(kernel, order), outs, [numbers], arrays, time)
        else:
            self.whole = line.run(name, whole_kernel, [(shape, BF)], [numbers], arrays, time)[0]
        self.step = 0
        if not self.fast:
            self.send = self.whole

    def go(self):
        if self.fast:
            self.other = self.line.swap(self.send, "seq", BITS[self.order[self.step]])

    def wait(self):
        if self.fast:
            self.line.wait(self.other)

    def join(self):
        self.step += 1
        if self.fast:
            count, *block = self.keep.shape
            kind = F32 if count == 2 else BF
            self.send, self.keep = self.line.run(
                f"{self.name}_join{self.step}",
                partial(join_kernel, self.order[self.step]),
                [((count // 2, *block), BF), ((count // 2, *block), kind)],
                [self.numbers],
                [self.other, self.keep],
            )

    def total(self, kind):
        if self.fast:
            block = self.keep.shape[1:]
            return self.line.run(self.name + "_sum", sum_kernel, [(block, kind)], [], [self.other, self.keep])[0]
        return lax.psum_scatter(
            self.whole, "seq", scatter_dimension=0 if self.blocks_first else 1, tiled=True
        ).astype(kind)


def normed_grad_kernel(pieces, w_mix, target):
    total = None
    count = pieces.shape[0]
    for j in range(count):
        for source, block in ((0, 0), (1, 3)):
            term = dot_nt(pieces[j, :, source * PAIR : (source + 1) * PAIR], columns_of(w_mix, block, j))
            total = term if total is None else total + term
    target[...] = total


def tokens_kernel(pieces, early, resid_grad, tokens, w_mix, target):
    total = early[...]
    count = pieces.shape[0]
    for j in range(count):
        for source, block in ((0, 1), (1, 2)):
            total = total + dot_nt(pieces[j, :, source * PAIR : (source + 1) * PAIR], columns_of(w_mix, block, j))
    target[...] = (resid_grad[...] + norm_back(tokens[...].astype(F32), total)).astype(BF)


def collect_kernel(numbers, *refs):
    early, late, mix, out = refs[1:5], (*refs[5:8], refs[0]), refs[8], refs[9]
    quarter = out.shape[1] // 4
    width = out.shape[1]
    owner = numbers[2]

    def pick(parts, j, block):
        columns = slice(block * quarter, (block + 1) * quarter)
        a, b, c, d = (parts[j ^ k][:, columns].astype(F32) for k in range(4))
        return jnp.where(owner < 2, jnp.where(owner == 0, a, b), jnp.where(owner == 2, c, d))

    for j in range(4):
        columns = lambda block: slice(block * width + j * quarter, block * width + (j + 1) * quarter)
        mix[:, columns(0)] = pick(early, j, 0)
        mix[:, columns(1)] = pick(late, j, 0)
        mix[:, columns(2)] = pick(late, j, 1)
        mix[:, columns(3)] = pick(early, j, 1)
        out[:, columns(0)] = pick(early, j, 2)


def on_device(tokens, lengths, forget, w_mix, w_out, w_gate, w_up, w_down, cotangent):
    shape = tokens.shape
    _, span, width = shape
    units = w_gate.shape[1]
    quarter = width // 4
    place = lax.axis_index("seq")
    owner = lax.axis_index("tp")
    numbers = jnp.stack([place % 2, place // 2, owner]).astype(jnp.int32)
    cosine, sine = rotation(place * span + jnp.arange(span, dtype=jnp.int32), HEAD)
    tokens = tokens.reshape(span, width)
    cotangent = cotangent.reshape(span, width)
    w_gate, w_up, w_down = w_gate.T, w_up.T, w_down.T
    small = (span, width)
    state = ((HALF, 2 * HEAD, HEAD), BF)
    line = Line()
    got = {}

    normed, raw_key, key, value, send, keep = line.run(
        "key_value",
        key_value_kernel,
        [(small, BF), (small, F32), ((span, 2 * width), BF), (small, BF), state, state],
        [numbers, forget],
        [tokens, cosine, sine, w_mix],
    )
    line.last = normed

    def fore_1(_):
        got["query"] = line.run(
            "query",
            query_kernel,
            [(small, F32), ((span, 2 * width), BF), (small, F32), ((HEADS, span, span), BF), (small, F32), (small, BF)],
            [numbers, lengths, forget],
            [normed, key, value, cosine, sine, w_mix, cotangent],
        )

    def fore_2(other):
        got["down_far"] = line.swap(got["query"][5], "tp", 2)

    def fore_3(near):
        got["normed_far"] = line.swap(normed, "tp", 2)
        got["down_near"] = line.swap(got["query"][5], "tp", 1)
        line.wait(got["down_far"], got["down_near"])

    def fore_4(far):
        got["down_cross"] = line.swap(got["down_far"], "tp", 1)
        line.wait(got["down_cross"], got["normed_far"])

    mine, theirs = scan(line, send, keep, numbers, forget, span, False, (fore_1, fore_2, fore_3, fore_4))
    raw_query, query, update, scores, intra, down_low = got["query"]
    down_rows = [down_low, got["down_near"], got["down_far"], got["down_cross"]]

    attention, gated, resid, ffn_in = line.run(
        "mix",
        mix_kernel,
        [(small, F32), (small, BF), (small, F32), (small, BF)],
        [numbers, forget],
        [theirs, mine, query, intra, update, tokens, w_out],
    )
    ffn_rows = [ffn_in, line.swap(ffn_in, "tp", 1), line.swap(ffn_in, "tp", 2)]
    normed_rows = [normed, line.swap(normed, "tp", 1), got["normed_far"], line.swap(got["normed_far"], "tp", 1)]
    gated_near = line.swap(gated, "tp", 1)
    hidden_grad = line.run(
        "hidden_grad", hidden_grad_kernel, [((2 * span, units), F32)] * 2, [], [*down_rows, w_down],
    )

    def ffn(name, first, second, upstream):
        return line.run(
            name,
            lambda rows_1, rows_0, *rest: ffn_kernel(rows_0, rows_1, *rest),
            [((2 * span, units), BF)] * 3 + [(small, BF)] * 2,
            [],
            [second, first, upstream, w_gate, w_up],
        )

    line.wait(normed_rows[1], normed_rows[3], gated_near)
    hidden_near, gate_near, up_near, back_0, back_1 = ffn("ffn_near", ffn_rows[0], ffn_rows[1], hidden_grad[0])
    ffn_rows.append(line.swap(ffn_rows[2], "tp", 1))
    hidden_far, gate_far, up_far, back_2, back_3 = ffn("ffn_far", ffn_rows[2], ffn_rows[3], hidden_grad[1])
    part_1, from_3 = line.swap(back_1, "tp", 1), line.swap(back_3, "tp", 1)

    def ffn_weight(name, order, near, far, rows, time=BRIEF):
        return Reduction(
            line, name, numbers, order, False, ffn_weight_kernel, whole_ffn_weight_kernel, (units, width),
            [near, far, *rows], time,
        )

    y_first, z_first = ("y", "z1", "z2"), ("z1", "y", "z2")
    gate_sum = ffn_weight("d_gate", y_first, gate_near, gate_far, ffn_rows)
    gate_sum.go()
    line.wait(part_1)
    part_2 = line.run("ffn_add", add_kernel, [(small, BF)], [], [from_3, back_2])[0]
    part_2 = line.swap(part_2, "tp", 2)
    down_sum = ffn_weight("d_down", z_first, hidden_near, hidden_far, down_rows)
    down_sum.go()
    downs = line.run(
        "down", down_kernel, [(small, BF)] * 4, [], [hidden_near, hidden_far, w_down],
    )
    down_1, down_3 = line.swap(downs[1], "tp", 1), line.swap(downs[3], "tp", 1)
    up_sum = ffn_weight("d_up", y_first, up_near, up_far, ffn_rows)
    resid_grad, mix_grad, update_grad, attention_grad, send, keep = line.run(
        "resid",
        resid_kernel,
        [(small, F32), (small, BF), (small, BF), (small, BF), state, state],
        [forget, numbers],
        [part_2, back_0, part_1, resid, down_low, attention, update, query, w_out],
    )

    def mix_weight(name, groups, arrays, columns, time=BRIEF):
        return Reduction(
            line, name, numbers, y_first, True,
            lambda order, *refs: mix_weight_kernel(groups, order, *refs),
            partial(whole_mix_weight_kernel, groups),
            (width, columns), arrays, time,
        )

    four, more, most = (0, 1, 2, 3), (4, 5, 6, 7), (8, 9, 10, 11)

    def back_1_(_):
        got["gated_far"] = line.swap(gated, "tp", 2)
        gate_sum.wait()
        line.wait(down_1, down_3)
        got["early"] = line.run(
            "early",
            early_kernel,
            [((span, 3 * quarter), BF)] * 4 + [(small, F32)] * 2 + [((4, span, 3 * quarter), BF)],
            [numbers, forget],
            [attention_grad, value, key, query, scores, theirs, mine, raw_query, cosine, sine, update_grad, mix_grad],
        )
        got["early_2"], got["early_3"] = line.swap(got["early"][2], "tp", 2), line.swap(got["early"][3], "tp", 3)
        got["down_2"] = line.run("down_add", add_kernel, [(small, BF)], [], [down_3, downs[2]])[0]
        down_sum.wait()

    def back_2_(other):
        up_sum.go()
        line.wait(got["gated_far"])

    def back_3_(near):
        got["gated_cross"] = line.swap(got["gated_far"], "tp", 1)
        up_sum.wait()
        line.wait(got["early_2"], got["early_3"], got["gated_cross"])

    def back_4_(far):
        got["early_1"] = line.swap(got["early"][1], "tp", 1)
        gate_sum.join()
        gate_sum.go()
        up_sum.join()
        up_sum.go()
        down_sum.join()
        got["normed_grad"] = line.run(
            "normed_grad", normed_grad_kernel, [(small, F32)], [], [got["early"][6], w_mix],
        )[0]
        got["early_sum"] = mix_weight(
            "d_early",
            [(most, four, 0, 2 * quarter), (more, four, 2 * quarter, 3 * quarter)],
            [got["early_1"], got["early"][0], got["early_2"], got["early_3"]]
            + [gated_near, gated, got["gated_far"], got["gated_cross"]]
            + [normed_rows[k] for k in (1, 0, 2, 3)],
            3 * quarter,
        )

    after_mine, after_theirs = scan(
        line, send, keep, numbers, forget, span, True, (back_1_, back_2_, back_3_, back_4_)
    )
    key_part, value_part = got["early"][4:6]
    early_sum = got["early_sum"]
    *late, late_pieces = line.run(
        "late",
        late_kernel,
        [((span, 2 * quarter), BF)] * 4 + [((4, span, 2 * quarter), BF)],
        [numbers, forget],
        [after_theirs, after_mine, value, key, raw_key, cosine, sine, key_part, value_part],
    )
    late_2, late_3 = line.swap(late[2], "tp", 2), line.swap(late[3], "tp", 3)
    late_1 = line.swap(late[1], "tp", 1)
    down_sum.go()
    early_sum.go()
    gate_sum.join()
    gate_sum.go()
    line.wait(late_2, late_3)
    late_sum = mix_weight(
        "d_late",
        [(more, four, 0, 2 * quarter)],
        [late_1, late[0], late_2, late_3] + [normed_rows[k] for k in (1, 0, 2, 3)],
        2 * quarter,
    )
    late_sum.go()
    up_sum.join()
    up_sum.go()
    down_2 = line.swap(got["down_2"], "tp", 2)
    gate_grad = gate_sum.total(F32)
    down_sum.join()
    down_sum.go()
    d_tokens = line.run(
        "d_tokens",
        tokens_kernel,
        [(small, BF)],
        [],
        [late_pieces, got["normed_grad"], resid_grad, tokens, w_mix],
    )[0]
    up_grad = up_sum.total(F32)
    early_sum.join()
    early_sum.go()
    out = line.run("out", out_kernel, [(small, BF)], [numbers, lengths], [down_2, downs[0], down_1, resid])[0]
    down_grad = down_sum.total(F32)
    early_sum.join()
    early_sum.go()
    late_sum.join()
    late_sum.go()
    early_all = early_sum.total(BF)
    early_full = [early_all, line.swap(early_all, "tp", 1), line.swap(early_all, "tp", 2)]
    late_sum.join()
    late_sum.go()
    late_all = late_sum.total(BF)
    early_full.append(line.swap(early_full[2], "tp", 1))
    late_full = [late_all, line.swap(late_all, "tp", 1), line.swap(late_all, "tp", 2)]
    late_full.append(swap(late_full[2], "tp", 1))
    rows = early_full[0].shape[0]
    mix_sum, out_sum = line.run(
        "collect",
        collect_kernel,
        [((rows, 4 * width), F32), ((rows, width), F32)],
        [numbers],
        [late_full[3], *early_full, *late_full[:3]],
    )
    return (out.reshape(shape), d_tokens.reshape(shape), mix_sum, out_sum, gate_grad.T, up_grad.T, down_grad.T)


def solution(mesh):
    in_specs = (
        P("tp", "seq", None),
        P(),
        P(),
        P(),
        P(),
        P(None, "tp"),
        P(None, "tp"),
        P(None, "tp"),
        P("tp", "seq", None),
    )
    out_specs = (
        P("tp", "seq", None),
        P("tp", "seq", None),
        P("seq", None),
        P("seq", None),
        P("seq", "tp"),
        P("seq", "tp"),
        P("seq", "tp"),
    )
    return jax.shard_map(
        on_device, mesh=mesh, in_specs=in_specs, out_specs=out_specs, check_vma=False
    )
```

profile of v0, /device:TPU:0, one launch (start us, length us, event | category | flops | bytes accessed | tf_op | source)
XLA Modules:
  0.0 228.7 jit_solution(17778146370847097481)
XLA Ops:
  2.0 3.4 %copy-done = bf16[1024,4096]{1,0:T(8,128)(2,1)S(1)} copy-done((bf16[1024,4096]{1,0:T(8,128)(2,1)S(1)}, bf16[1024,4096]{1,0:T(8,128)(2,1)}, u32[]{:S(2)}) %copy-start) | copy-done | bytes 8388632
  7.1 3.1 %key_value.1 = (bf16[256,1024]{1,0:T(8,128)(2,1)S(1)}, f32[256,1024]{1,0:T(8,128)S(1)}, bf16[256,2048]{1,0:T(8,128)(2,1)S(1)}, bf16[256,1024]{1,0:T(8,128)(2,1)S...) custom-call(s32[3]{0:T(128)S(1)} %pad_add_fusion.numbers.refs_0_, f32[8]{0:T(128)S(1)} %copy-done.9, ...), custom_call_target="tpu_custom_call" | custom-call | flops 22000000 | bytes 1024 | tf_op jit(solution)/shard_map/key_value/pallas_call | solution.py:122
  10.2 3.0 %collective-permute-start = (bf16[4,256,128]{2,1,0:T(8,128)(2,1)S(1)}, bf16[4,256,128]{2,1,0:T(8,128)(2,1)S(1)}, u32[]{:S(2)}, u32[]{:S(2)}) collective-permute-start(bf16[4,256,128]{2,1,0:T(8,128)(2,1)S(1)} %get-tuple-element.191), channel_id=1, source_target_pairs={{0,4},{4,0},{8,12},{12,8},{16,20},{20,16},{24,28},{28,24},{1,5},{5... | collective-permute-start | bytes 786440 | tf_op jit(solution)/shard_map/ppermute | solution.py:59
  13.2 2.8 %query.1 = (f32[256,1024]{1,0:T(8,128)S(1)}, bf16[256,2048]{1,0:T(8,128)(2,1)S(1)}, f32[256,1024]{1,0:T(8,128)S(1)}, bf16[8,256,256]{2,1,0:T(8,128)(2,1)S(1)}, f...) custom-call(s32[3]{0:T(128)S(1)} %pad_add_fusion.numbers.refs_0_, s32[4]{0:T(128)S(1)} %copy-done.11, ...), custom_call_target="tpu_custom_call" | custom-call | flops 22000000 | bytes 1024 | tf_op jit(solution)/shard_map/query/pallas_call | solution.py:122
  16.1 3.5 %collective-permute-done.other = bf16[4,256,128]{2,1,0:T(8,128)(2,1)S(1)} collective-permute-done((bf16[4,256,128]{2,1,0:T(8,128)(2,1)S(1)}, bf16[4,256,128]{2,1,0:T(8,128)(2,1)S(1)}, u32[]{:S(2)}, u32[]{:S(2)}) %collective-permute-start) | collective-permute-done | bytes 262176 | tf_op jit(solution)/shard_map/ppermute | solution.py:59
  20.2 1.9 collective-permute-start.1
  23.5 4.2 %collective-permute-done.1.near = bf16[4,256,128]{2,1,0:T(8,128)(2,1)S(1)} collective-permute-done((bf16[4,256,128]{2,1,0:T(8,128)(2,1)S(1)}, bf16[4,256,128]{2,1,0:T(8,128)(2,1)S(1)}, u32[]{:S(2)}, u32[]{:S(2)}) %collective-permute-start.1) | collective-permute-done | bytes 262176 | tf_op jit(solution)/shard_map/ppermute | solution.py:59
  28.5 2.6 %collective-permute-start.4 = (bf16[4,256,128]{2,1,0:T(8,128)(2,1)S(1)}, bf16[4,256,128]{2,1,0:T(8,128)(2,1)S(1)}, u32[]{:S(2)}, u32[]{:S(2)}) collective-permute-start(bf16[4,256,128]{2,1,0:T(8,128)(2,1)S(1)} %fore_quad.1), channel_id=1, source_target_pairs={{0,16},{4,20},{8,24},{12,28},{16,0},{20,4},{24,8},{28,12},{1,17},{... | collective-permute-start | bytes 786440 | tf_op jit(solution)/shard_map/ppermute | solution.py:59
  32.5 2.7 %collective-permute-done.2.rows_2.refs_4_ = bf16[256,1024]{1,0:T(8,128)(2,1)S(1)} collective-permute-done((bf16[256,1024]{1,0:T(8,128)(2,1)S(1)}, bf16[256,1024]{1,0:T(8,128)(2,1)S(1)}, u32[]{:S(2)}, u32[]{:S(2)}) %collective-permute-start.2) | collective-permute-done | bytes 524320 | tf_op jit(solution)/shard_map/ppermute | solution.py:59
  35.3 8.5 %collective-permute-done.4.far = bf16[4,256,128]{2,1,0:T(8,128)(2,1)S(1)} collective-permute-done((bf16[4,256,128]{2,1,0:T(8,128)(2,1)S(1)}, bf16[4,256,128]{2,1,0:T(8,128)(2,1)S(1)}, u32[]{:S(2)}, u32[]{:S(2)}) %collective-permute-start.4) | collective-permute-done | bytes 262176 | tf_op jit(solution)/shard_map/ppermute | solution.py:59
  46.1 7.2 %collective-permute-done.5.theirs = bf16[4,256,128]{2,1,0:T(8,128)(2,1)S(1)} collective-permute-done((bf16[4,256,128]{2,1,0:T(8,128)(2,1)S(1)}, bf16[4,256,128]{2,1,0:T(8,128)(2,1)S(1)}, u32[]{:S(2)}, u32[]{:S(2)}) %collective-permute-start.5) | collective-permute-done | bytes 262176 | tf_op jit(solution)/shard_map/ppermute | solution.py:59
  53.4 2.0 mix.1
  57.8 1.8 hidden_grad.1
  59.7 3.6 %ffn_near.1 = (bf16[512,704]{1,0:T(8,128)(2,1)S(1)}, bf16[512,704]{1,0:T(8,128)(2,1)S(1)}, bf16[512,704]{1,0:T(8,128)(2,1)S(1)}, bf16[256,1024]{1,0:T(8,128)(2,1)S(1)}, bf16[256,1024]{1,0:T(8,128)(2,1)S(1)}) custom-call(bf16[256,1024]{1,0:T(8,128)(2,1)S(1)} %collective-permute-done.8.rows_1.refs_3_, bf16[256,1024]{1,0:T(8,128)(2,1)S(1)} %get-tuple-element.209.rows_0.refs_2_, ...), custom_call_target="tpu_custom_call" | custom-call | flops 22000000 | bytes 1024 | tf_op jit(solution)/shard_map/ffn_near/pallas_call | solution.py:122
  63.3 7.0 %collective-permute-done.12.rows_0.refs_4_ = bf16[256,1024]{1,0:T(8,128)(2,1)S(1)} collective-permute-done((bf16[256,1024]{1,0:T(8,128)(2,1)S(1)}, bf16[256,1024]{1,0:T(8,128)(2,1)S(1)}, u32[]{:S(2)}, u32[]{:S(2)}) %collective-permute-start.12) | collective-permute-done | bytes 524320 | tf_op jit(solution)/shard_map/ppermute | solution.py:59
  70.3 1.9 collective-permute-done.13.rows_1.refs_5_
  72.2 3.9 %ffn_far.1 = (bf16[512,704]{1,0:T(8,128)(2,1)S(1)}, bf16[512,704]{1,0:T(8,128)(2,1)S(1)}, bf16[512,704]{1,0:T(8,128)(2,1)S(1)}, bf16[256,1024]{1,0:T(8,128)(2,1)S(1)}, bf16[256,1024]{1,0:T(8,128)(2,1)S(1)}) custom-call(bf16[256,1024]{1,0:T(8,128)(2,1)S(1)} %collective-permute-done.13.rows_1.refs_5_, ...), custom_call_target="tpu_custom_call" | custom-call | flops 22000000 | bytes 1024 | tf_op jit(solution)/shard_map/ffn_far/pallas_call | solution.py:122
  76.7 2.2 d_gate.1
  80.5 1.5 collective-permute-start.17
  82.1 2.2 d_down.1
  85.1 1.8 down.1
  87.5 2.2 d_up.1
  89.7 4.6 %collective-permute-done.17.part_0 = bf16[256,1024]{1,0:T(8,128)(2,1)S(1)} collective-permute-done((bf16[256,1024]{1,0:T(8,128)(2,1)S(1)}, bf16[256,1024]{1,0:T(8,128)(2,1)S(1)}, u32[]{:S(2)}, u32[]{:S(2)}) %collective-permute-start.17) | collective-permute-done | bytes 524320 | tf_op jit(solution)/shard_map/ppermute | solution.py:59
  94.3 2.6 %resid.1 = (f32[256,1024]{1,0:T(8,128)S(1)}, bf16[256,1024]{1,0:T(8,128)(2,1)S(1)}, bf16[256,1024]{1,0:T(8,128)(2,1)S(1)}, bf16[256,1024]{1,0:T(8,128)(2,1)S(1)}...) custom-call(f32[8]{0:T(128)S(1)} %copy-done.10, s32[3]{0:T(128)S(1)} %pad_add_fusion.numbers.refs_0_, ...), custom_call_target="tpu_custom_call" | custom-call | flops 22000000 | bytes 1024 | tf_op jit(solution)/shard_map/resid/pallas_call | solution.py:122
  99.0 12.4 %early.1 = (bf16[256,768]{1,0:T(8,128)(2,1)S(1)}, bf16[256,768]{1,0:T(8,128)(2,1)S(1)}, bf16[256,768]{1,0:T(8,128)(2,1)S(1)}, bf16[256,768]{1,0:T(8,128)(2,1)S(1...) custom-call(s32[3]{0:T(128)S(1)} %pad_add_fusion.numbers.refs_0_, ...), custom_call_target="tpu_custom_call" | custom-call | flops 22000000 | bytes 1024 | tf_op jit(solution)/shard_map/early/pallas_call | solution.py:122
  112.9 1.5 collective-permute-start.22
  114.5 4.5 %collective-permute-done.23.near = bf16[4,256,128]{2,1,0:T(8,128)(2,1)S(1)} collective-permute-done((bf16[4,256,128]{2,1,0:T(8,128)(2,1)S(1)}, bf16[4,256,128]{2,1,0:T(8,128)(2,1)S(1)}, u32[]{:S(2)}, u32[]{:S(2)}) %collective-permute-start.23) | collective-permute-done | bytes 262176 | tf_op jit(solution)/shard_map/ppermute | solution.py:59
  121.6 2.3 %collective-permute-start.28 = (bf16[4,256,128]{2,1,0:T(8,128)(2,1)S(1)}, bf16[4,256,128]{2,1,0:T(8,128)(2,1)S(1)}, u32[]{:S(2)}, u32[]{:S(2)}) collective-permute-start(bf16[4,256,128]{2,1,0:T(8,128)(2,1)S(1)} %back_quad.1), channel_id=1, source_target_pairs={{0,16},{4,20},{8,24},{12,28},{16,0},{20,4},{24,8},{28,12},{1,17},{... | collective-permute-start | bytes 786440 | tf_op jit(solution)/shard_map/ppermute | solution.py:59
  123.9 7.8 %collective-permute-done.25.refs_3_ = bf16[256,768]{1,0:T(8,128)(2,1)S(1)} collective-permute-done((bf16[256,768]{1,0:T(8,128)(2,1)S(1)}, bf16[256,768]{1,0:T(8,128)(2,1)S(1)}, u32[]{:S(2)}, u32[]{:S(2)}) %collective-permute-start.25) | collective-permute-done | bytes 393248 | tf_op jit(solution)/shard_map/ppermute | solution.py:59
  131.7 7.5 %collective-permute-done.26.refs_4_ = bf16[256,768]{1,0:T(8,128)(2,1)S(1)} collective-permute-done((bf16[256,768]{1,0:T(8,128)(2,1)S(1)}, bf16[256,768]{1,0:T(8,128)(2,1)S(1)}, u32[]{:S(2)}, u32[]{:S(2)}) %collective-permute-start.26) | collective-permute-done | bytes 393248 | tf_op jit(solution)/shard_map/ppermute | solution.py:59
  146.2 2.5 %d_early.1 = (bf16[4,128,768]{2,1,0:T(8,128)(2,1)S(1)}, bf16[4,128,768]{2,1,0:T(8,128)(2,1)S(1)}) custom-call(s32[3]{0:T(128)S(1)} %pad_add_fusion.numbers.refs_0_, bf16[256,768]{1,0:T(8,128)(2,1)S(1)} %collective-permute-done.31.refs_1_, bf16[256,768]{1,0:T(8,128)(2,1)S(1)} %get-tuple-element.258.refs_2_, ...), custom_call_target="tpu_custom_call" | custom-call | flops 22000000 | bytes 1024 | tf_op jit(solution)/shard_map/d_early/pallas_call | solution.py:122
  148.8 1.7 late.1
  150.6 1.6 collective-permute-start.37
  156.0 5.2 %collective-permute-done.34.refs_3_ = bf16[256,512]{1,0:T(8,128)(2,1)S(1)} collective-permute-done((bf16[256,512]{1,0:T(8,128)(2,1)S(1)}, bf16[256,512]{1,0:T(8,128)(2,1)S(1)}, u32[]{:S(2)}, u32[]{:S(2)}) %collective-permute-start.34) | collective-permute-done | bytes 262176 | tf_op jit(solution)/shard_map/ppermute | solution.py:59
  161.2 2.3 %collective-permute-start.40 = (bf16[1,704,128]{2,1,0:T(8,128)(2,1)S(1)}, bf16[1,704,128]{2,1,0:T(8,128)(2,1)S(1)}, u32[]{:S(2)}, u32[]{:S(2)}) collective-permute-start(bf16[1,704,128]{2,1,0:T(8,128)(2,1)S(1)} %get-tuple-element.321), channel_id=1, source_target_pairs={{0,16},{4,20},{8,24},{12,28},{16,0},{20,4},{24,8},{28,12},{1,17},{... | collective-permute-start | bytes 540680 | tf_op jit(solution)/shard_map/ppermute | solution.py:59
  163.6 2.5 %collective-permute-done.35.refs_4_ = bf16[256,512]{1,0:T(8,128)(2,1)S(1)} collective-permute-done((bf16[256,512]{1,0:T(8,128)(2,1)S(1)}, bf16[256,512]{1,0:T(8,128)(2,1)S(1)}, u32[]{:S(2)}, u32[]{:S(2)}) %collective-permute-start.35) | collective-permute-done | bytes 262176 | tf_op jit(solution)/shard_map/ppermute | solution.py:59
  166.1 1.8 d_late.1
  168.6 2.4 %collective-permute-start.38 = (bf16[1,704,128]{2,1,0:T(8,128)(2,1)S(1)}, bf16[1,704,128]{2,1,0:T(8,128)(2,1)S(1)}, u32[]{:S(2)}, u32[]{:S(2)}) collective-permute-start(bf16[1,704,128]{2,1,0:T(8,128)(2,1)S(1)} %get-tuple-element.318), channel_id=1, source_target_pairs={{0,16},{4,20},{8,24},{12,28},{16,0},{20,4},{24,8},{28,12},{1,17},{... | collective-permute-start | bytes 540680 | tf_op jit(solution)/shard_map/ppermute | solution.py:59
  173.6 5.2 %collective-permute-done.39.other = bf16[2,704,128]{2,1,0:T(8,128)(2,1)S(1)} collective-permute-done((bf16[2,704,128]{2,1,0:T(8,128)(2,1)S(1)}, bf16[2,704,128]{2,1,0:T(8,128)(2,1)S(1)}, u32[]{:S(2)}, u32[]{:S(2)}) %collective-permute-start.39) | collective-permute-done | bytes 360480 | tf_op jit(solution)/shard_map/ppermute | solution.py:59
  179.5 2.4 %d_tokens.1 = bf16[256,1024]{1,0:T(8,128)(2,1)} custom-call(bf16[4,256,512]{2,1,0:T(8,128)(2,1)S(1)} %get-tuple-element.327.pieces, f32[256,1024]{1,0:T(8,128)S(1)} %normed_grad.1.early, f32[256,1024]{1,0:T(8,128)S(1)} %get-tuple-element.249.resid_grad, bf16[256,1024]{1,0:T(8,128)(2,1)S(1)} %bitcast.21, bf16[1024,4096]{1,0:T(8,128)(2,1)S(1)} %copy-done.1), custom_call_target="tpu_custom_call" | custom-call | flops 22000000 | bytes 1024 | tf_op jit(solution)/shard_map/d_tokens/pallas_call | solution.py:122
  184.5 2.9 %collective-permute-start.43 = (bf16[1,704,128]{2,1,0:T(8,128)(2,1)S(1)}, bf16[1,704,128]{2,1,0:T(8,128)(2,1)S(1)}, u32[]{:S(2)}, u32[]{:S(2)}) collective-permute-start(bf16[1,704,128]{2,1,0:T(8,128)(2,1)S(1)} %get-tuple-element.336), channel_id=1, source_target_pairs={{0,16},{4,20},{8,24},{12,28},{16,0},{20,4},{24,8},{28,12},{1,17},{... | collective-permute-start | bytes 540680 | tf_op jit(solution)/shard_map/ppermute | solution.py:59
  187.5 1.6 out.1
  189.1 5.7 %collective-permute-done.43.other = bf16[1,704,128]{2,1,0:T(8,128)(2,1)S(1)} collective-permute-done((bf16[1,704,128]{2,1,0:T(8,128)(2,1)S(1)}, bf16[1,704,128]{2,1,0:T(8,128)(2,1)S(1)}, u32[]{:S(2)}, u32[]{:S(2)}) %collective-permute-start.43) | collective-permute-done | bytes 180256 | tf_op jit(solution)/shard_map/ppermute | solution.py:59
  197.9 3.2 %collective-permute-start.44 = (bf16[2,128,512]{2,1,0:T(8,128)(2,1)S(1)}, bf16[2,128,512]{2,1,0:T(8,128)(2,1)S(1)}, u32[]{:S(2)}, u32[]{:S(2)}) collective-permute-start(bf16[2,128,512]{2,1,0:T(8,128)(2,1)S(1)} %get-tuple-element.345), channel_id=1, source_target_pairs={{0,8},{4,12},{8,0},{12,4},{16,24},{20,28},{24,16},{28,20},{1,9},{5... | collective-permute-start | bytes 786440 | tf_op jit(solution)/shard_map/ppermute | solution.py:59
  202.1 9.7 %collective-permute-done.45.other = bf16[1,128,768]{2,1,0:T(8,128)(2,1)S(1)} collective-permute-done((bf16[1,128,768]{2,1,0:T(8,128)(2,1)S(1)}, bf16[1,128,768]{2,1,0:T(8,128)(2,1)S(1)}, u32[]{:S(2)}, u32[]{:S(2)}) %collective-permute-start.45) | collective-permute-done | bytes 196640 | tf_op jit(solution)/shard_map/ppermute | solution.py:59
  213.1 6.2 %collective-permute-done.46.other = bf16[1,128,512]{2,1,0:T(8,128)(2,1)S(1)} collective-permute-done((bf16[1,128,512]{2,1,0:T(8,128)(2,1)S(1)}, bf16[1,128,512]{2,1,0:T(8,128)(2,1)S(1)}, u32[]{:S(2)}, u32[]{:S(2)}) %collective-permute-start.46) | collective-permute-done | bytes 131104 | tf_op jit(solution)/shard_map/ppermute | solution.py:59
  220.4 3.9 %collective-permute-done.47.refs_7_ = bf16[128,512]{1,0:T(8,128)(2,1)S(1)} collective-permute-done((bf16[128,512]{1,0:T(8,128)(2,1)S(1)}, bf16[128,512]{1,0:T(8,128)(2,1)S(1)}, u32[]{:S(2)}, u32[]{:S(2)}) %collective-permute-start.47) | collective-permute-done | bytes 131104 | tf_op jit(solution)/shard_map/ppermute | solution.py:59
  225.9 2.6 %collect.1 = (f32[128,4096]{1,0:T(8,128)}, f32[128,1024]{1,0:T(8,128)}) custom-call(s32[3]{0:T(128)S(1)} %pad_add_fusion.numbers.refs_0_, bf16[128,512]{1,0:T(8,128)(2,1)S(1)} %collective-permute-done.48.refs_0_, bf16[128,768]{1,0:T(8,128)(2,1)S(1)} %d_early_sum.1.refs_1_, bf16[128,768]{1,0:T(8,128)(2,1)S(1)} %collective-permute-done.49.refs_2_, ...), custom_call_target="tpu_custom_call" | custom-call | flops 22000000 | bytes 1024 | tf_op jit(solution)/shard_map/collect/pallas_call | solution.py:122
  (127 shorter events, 47.6 us)
Async XLA Ops:
  10.2 9.3 %collective-permute-start = (bf16[4,256,128]{2,1,0:T(8,128)(2,1)S(1)}, bf16[4,256,128]{2,1,0:T(8,128)(2,1)S(1)}, u32[]{:S(2)}, u32[]{:S(2)}) collective-permute-start(bf16[4,256,128]{2,1,0:T(8,128)(2,1)S(1)} %get-tuple-element.191), channel_id=1, source_target_pairs={{0,4},{4,0},{8,12},{12,8},{16,20},{20,16},{24,28},{28,24},{1,5},{5... | collective-permute-start | bytes 786440 | tf_op jit(solution)/shard_map/ppermute | solution.py:59
  20.2 7.6 %collective-permute-start.1 = (bf16[4,256,128]{2,1,0:T(8,128)(2,1)S(1)}, bf16[4,256,128]{2,1,0:T(8,128)(2,1)S(1)}, u32[]{:S(2)}, u32[]{:S(2)}) collective-permute-start(bf16[4,256,128]{2,1,0:T(8,128)(2,1)S(1)} %fore_pair.1.pair), channel_id=1, source_target_pairs={{0,8},{4,12},{8,0},{12,4},{16,24},{20,28},{24,16},{28,20},{1,9},{5... | collective-permute-start | bytes 786440 | tf_op jit(solution)/shard_map/ppermute | solution.py:59
  22.1 13.2 %collective-permute-start.2 = (bf16[256,1024]{1,0:T(8,128)(2,1)S(1)}, bf16[256,1024]{1,0:T(8,128)(2,1)S(1)}, u32[]{:S(2)}, u32[]{:S(2)}) collective-permute-start(bf16[256,1024]{1,0:T(8,128)(2,1)S(1)} %get-tuple-element.210.rows_0.refs_2_.down_low), channel_id=1, source_target_pairs={{0,2},{1,3},{2,0},{3,1},{4,6},{5,7},{6,4},{7,5},{8,10},{9,11},{10,... | collective-permute-start | bytes 1572872 | tf_op jit(solution)/shard_map/ppermute | solution.py:59
  28.4 6.9 %collective-permute-start.3 = (bf16[256,1024]{1,0:T(8,128)(2,1)S(1)}, bf16[256,1024]{1,0:T(8,128)(2,1)S(1)}, u32[]{:S(2)}, u32[]{:S(2)}) collective-permute-start(bf16[256,1024]{1,0:T(8,128)(2,1)S(1)} %get-tuple-element.210.rows_0.refs_2_.down_low), channel_id=1, source_target_pairs={{0,1},{1,0},{2,3},{3,2},{4,5},{5,4},{6,7},{7,6},{8,9},{9,8},{10,11... | collective-permute-start | bytes 1572872 | tf_op jit(solution)/shard_map/ppermute | solution.py:59
  28.5 15.2 %collective-permute-start.4 = (bf16[4,256,128]{2,1,0:T(8,128)(2,1)S(1)}, bf16[4,256,128]{2,1,0:T(8,128)(2,1)S(1)}, u32[]{:S(2)}, u32[]{:S(2)}) collective-permute-start(bf16[4,256,128]{2,1,0:T(8,128)(2,1)S(1)} %fore_quad.1), channel_id=1, source_target_pairs={{0,16},{4,20},{8,24},{12,28},{16,0},{20,4},{24,8},{28,12},{1,17},{... | collective-permute-start | bytes 786440 | tf_op jit(solution)/shard_map/ppermute | solution.py:59
  31.0 22.3 %collective-permute-start.7 = (bf16[256,1024]{1,0:T(8,128)(2,1)S(1)}, bf16[256,1024]{1,0:T(8,128)(2,1)S(1)}, u32[]{:S(2)}, u32[]{:S(2)}) collective-permute-start(bf16[256,1024]{1,0:T(8,128)(2,1)S(1)} %get-tuple-element.213.normed.refs_10_.refs_6_), channel_id=1, source_target_pairs={{0,2},{1,3},{2,0},{3,1},{4,6},{5,7},{6,4},{7,5},{8,10},{9,11},{10,... | collective-permute-start | bytes 1572872 | tf_op jit(solution)/shard_map/ppermute | solution.py:59
  44.5 8.8 %collective-permute-start.6 = (bf16[256,1024]{1,0:T(8,128)(2,1)S(1)}, bf16[256,1024]{1,0:T(8,128)(2,1)S(1)}, u32[]{:S(2)}, u32[]{:S(2)}) collective-permute-start(bf16[256,1024]{1,0:T(8,128)(2,1)S(1)} %collective-permute-done.2.rows_2.refs_4_), channel_id=1, source_target_pairs={{0,1},{1,0},{2,3},{3,2},{4,5},{5,4},{6,7},{7,6},{8,9},{9,8},{10,11... | collective-permute-start | bytes 1572872 | tf_op jit(solution)/shard_map/ppermute | solution.py:59
  44.6 8.7 %collective-permute-start.5 = (bf16[4,256,128]{2,1,0:T(8,128)(2,1)S(1)}, bf16[4,256,128]{2,1,0:T(8,128)(2,1)S(1)}, u32[]{:S(2)}, u32[]{:S(2)}) collective-permute-start(bf16[4,256,128]{2,1,0:T(8,128)(2,1)S(1)} %get-tuple-element.198), channel_id=1, source_target_pairs={{0,4},{4,0},{8,12},{12,8},{16,20},{20,16},{24,28},{28,24},{1,5},{5... | collective-permute-start | bytes 786440 | tf_op jit(solution)/shard_map/ppermute | solution.py:59
  55.3 4.3 %collective-permute-start.8 = (bf16[256,1024]{1,0:T(8,128)(2,1)S(1)}, bf16[256,1024]{1,0:T(8,128)(2,1)S(1)}, u32[]{:S(2)}, u32[]{:S(2)}) collective-permute-start(bf16[256,1024]{1,0:T(8,128)(2,1)S(1)} %get-tuple-element.209.rows_0.refs_2_), channel_id=1, source_target_pairs={{0,1},{1,0},{2,3},{3,2},{4,5},{5,4},{6,7},{7,6},{8,9},{9,8},{10,11... | collective-permute-start | bytes 1572872 | tf_op jit(solution)/shard_map/ppermute | solution.py:59
  55.4 4.3 %collective-permute-start.9 = (bf16[256,1024]{1,0:T(8,128)(2,1)S(1)}, bf16[256,1024]{1,0:T(8,128)(2,1)S(1)}, u32[]{:S(2)}, u32[]{:S(2)}) collective-permute-start(bf16[256,1024]{1,0:T(8,128)(2,1)S(1)} %get-tuple-element.213.normed.refs_10_.refs_6_), channel_id=1, source_target_pairs={{0,1},{1,0},{2,3},{3,2},{4,5},{5,4},{6,7},{7,6},{8,9},{9,8},{10,11... | collective-permute-start | bytes 1572872 | tf_op jit(solution)/shard_map/ppermute | solution.py:59
  55.9 3.8 %collective-permute-start.10 = (bf16[256,1024]{1,0:T(8,128)(2,1)S(1)}, bf16[256,1024]{1,0:T(8,128)(2,1)S(1)}, u32[]{:S(2)}, u32[]{:S(2)}) collective-permute-start(bf16[256,1024]{1,0:T(8,128)(2,1)S(1)} %collective-permute-done.7.refs_11_.refs_7_), channel_id=1, source_target_pairs={{0,1},{1,0},{2,3},{3,2},{4,5},{5,4},{6,7},{7,6},{8,9},{9,8},{10,11... | collective-permute-start | bytes 1572872 | tf_op jit(solution)/shard_map/ppermute | solution.py:59
  56.4 13.9 %collective-permute-start.12 = (bf16[256,1024]{1,0:T(8,128)(2,1)S(1)}, bf16[256,1024]{1,0:T(8,128)(2,1)S(1)}, u32[]{:S(2)}, u32[]{:S(2)}) collective-permute-start(bf16[256,1024]{1,0:T(8,128)(2,1)S(1)} %get-tuple-element.209.rows_0.refs_2_), channel_id=1, source_target_pairs={{0,2},{1,3},{2,0},{3,1},{4,6},{5,7},{6,4},{7,5},{8,10},{9,11},{10,... | collective-permute-start | bytes 1572872 | tf_op jit(solution)/shard_map/ppermute | solution.py:59
  76.1 4.3 %collective-permute-start.14 = (bf16[256,1024]{1,0:T(8,128)(2,1)S(1)}, bf16[256,1024]{1,0:T(8,128)(2,1)S(1)}, u32[]{:S(2)}, u32[]{:S(2)}) collective-permute-start(bf16[256,1024]{1,0:T(8,128)(2,1)S(1)} %get-tuple-element.224), channel_id=1, source_target_pairs={{0,1},{1,0},{2,3},{3,2},{4,5},{5,4},{6,7},{7,6},{8,9},{9,8},{10,11... | collective-permute-start | bytes 1572872 | tf_op jit(solution)/shard_map/ppermute | solution.py:59
  76.3 4.1 %collective-permute-start.15 = (bf16[256,1024]{1,0:T(8,128)(2,1)S(1)}, bf16[256,1024]{1,0:T(8,128)(2,1)S(1)}, u32[]{:S(2)}, u32[]{:S(2)}) collective-permute-start(bf16[256,1024]{1,0:T(8,128)(2,1)S(1)} %get-tuple-element.231), channel_id=1, source_target_pairs={{0,1},{1,0},{2,3},{3,2},{4,5},{5,4},{6,7},{7,6},{8,9},{9,8},{10,11... | collective-permute-start | bytes 1572872 | tf_op jit(solution)/shard_map/ppermute | solution.py:59
  78.9 18.7 %collective-permute-start.18 = (bf16[4,704,128]{2,1,0:T(8,128)(2,1)S(1)}, bf16[4,704,128]{2,1,0:T(8,128)(2,1)S(1)}, u32[]{:S(2)}, u32[]{:S(2)}) collective-permute-start(bf16[4,704,128]{2,1,0:T(8,128)(2,1)S(1)} %get-tuple-element.251), channel_id=1, source_target_pairs={{0,4},{4,0},{8,12},{12,8},{16,20},{20,16},{24,28},{28,24},{1,5},{5... | collective-permute-start | bytes 2162696 | tf_op jit(solution)/shard_map/ppermute | solution.py:59
  80.5 13.8 %collective-permute-start.17 = (bf16[256,1024]{1,0:T(8,128)(2,1)S(1)}, bf16[256,1024]{1,0:T(8,128)(2,1)S(1)}, u32[]{:S(2)}, u32[]{:S(2)}) collective-permute-start(bf16[256,1024]{1,0:T(8,128)(2,1)S(1)} %ffn_add.1), channel_id=1, source_target_pairs={{0,2},{1,3},{2,0},{3,1},{4,6},{5,7},{6,4},{7,5},{8,10},{9,11},{10,... | collective-permute-start | bytes 1572872 | tf_op jit(solution)/shard_map/ppermute | solution.py:59
  84.3 27.2 %collective-permute-start.20 = (bf16[4,704,128]{2,1,0:T(8,128)(2,1)S(1)}, bf16[4,704,128]{2,1,0:T(8,128)(2,1)S(1)}, u32[]{:S(2)}, u32[]{:S(2)}) collective-permute-start(bf16[4,704,128]{2,1,0:T(8,128)(2,1)S(1)} %get-tuple-element.263), channel_id=1, source_target_pairs={{0,8},{4,12},{8,0},{12,4},{16,24},{20,28},{24,16},{28,20},{1,9},{5... | collective-permute-start | bytes 2162696 | tf_op jit(solution)/shard_map/ppermute | solution.py:59
  86.9 12.1 %collective-permute-start.16 = (bf16[256,1024]{1,0:T(8,128)(2,1)S(1)}, bf16[256,1024]{1,0:T(8,128)(2,1)S(1)}, u32[]{:S(2)}, u32[]{:S(2)}) collective-permute-start(bf16[256,1024]{1,0:T(8,128)(2,1)S(1)} %get-tuple-element.239), channel_id=1, source_target_pairs={{0,1},{1,0},{2,3},{3,2},{4,5},{5,4},{6,7},{7,6},{8,9},{9,8},{10,11... | collective-permute-start | bytes 1572872 | tf_op jit(solution)/shard_map/ppermute | solution.py:59
  87.0 12.0 %collective-permute-start.19 = (bf16[256,1024]{1,0:T(8,128)(2,1)S(1)}, bf16[256,1024]{1,0:T(8,128)(2,1)S(1)}, u32[]{:S(2)}, u32[]{:S(2)}) collective-permute-start(bf16[256,1024]{1,0:T(8,128)(2,1)S(1)} %get-tuple-element.253), channel_id=1, source_target_pairs={{0,1},{1,0},{2,3},{3,2},{4,5},{5,4},{6,7},{7,6},{8,9},{9,8},{10,11... | collective-permute-start | bytes 1572872 | tf_op jit(solution)/shard_map/ppermute | solution.py:59
  96.9 14.6 %collective-permute-start.21 = (bf16[4,256,128]{2,1,0:T(8,128)(2,1)S(1)}, bf16[4,256,128]{2,1,0:T(8,128)(2,1)S(1)}, u32[]{:S(2)}, u32[]{:S(2)}) collective-permute-start(bf16[4,256,128]{2,1,0:T(8,128)(2,1)S(1)} %get-tuple-element.265), channel_id=1, source_target_pairs={{0,4},{4,0},{8,12},{12,8},{16,20},{20,16},{24,28},{28,24},{1,5},{5... | collective-permute-start | bytes 786440 | tf_op jit(solution)/shard_map/ppermute | solution.py:59
  97.6 16.9 %collective-permute-start.24 = (bf16[256,1024]{1,0:T(8,128)(2,1)S(1)}, bf16[256,1024]{1,0:T(8,128)(2,1)S(1)}, u32[]{:S(2)}, u32[]{:S(2)}) collective-permute-start(bf16[256,1024]{1,0:T(8,128)(2,1)S(1)} %get-tuple-element.268.refs_6_), channel_id=1, source_target_pairs={{0,2},{1,3},{2,0},{3,1},{4,6},{5,7},{6,4},{7,5},{8,10},{9,11},{10,... | collective-permute-start | bytes 1572872 | tf_op jit(solution)/shard_map/ppermute | solution.py:59
  112.2 6.8 %collective-permute-start.23 = (bf16[4,256,128]{2,1,0:T(8,128)(2,1)S(1)}, bf16[4,256,128]{2,1,0:T(8,128)(2,1)S(1)}, u32[]{:S(2)}, u32[]{:S(2)}) collective-permute-start(bf16[4,256,128]{2,1,0:T(8,128)(2,1)S(1)} %back_pair.1.pair), channel_id=1, source_target_pairs={{0,8},{4,12},{8,0},{12,4},{16,24},{20,28},{24,16},{28,20},{1,9},{5... | collective-permute-start | bytes 786440 | tf_op jit(solution)/shard_map/ppermute | solution.py:59
  112.9 26.3 %collective-permute-start.22 = (bf16[4,704,128]{2,1,0:T(8,128)(2,1)S(1)}, bf16[4,704,128]{2,1,0:T(8,128)(2,1)S(1)}, u32[]{:S(2)}, u32[]{:S(2)}) collective-permute-start(bf16[4,704,128]{2,1,0:T(8,128)(2,1)S(1)} %get-tuple-element.266), channel_id=1, source_target_pairs={{0,4},{4,0},{8,12},{12,8},{16,20},{20,16},{24,28},{28,24},{1,5},{5... | collective-permute-start | bytes 2162696 | tf_op jit(solution)/shard_map/ppermute | solution.py:59
  119.7 19.6 %collective-permute-start.27 = (bf16[256,1024]{1,0:T(8,128)(2,1)S(1)}, bf16[256,1024]{1,0:T(8,128)(2,1)S(1)}, u32[]{:S(2)}, u32[]{:S(2)}) collective-permute-start(bf16[256,1024]{1,0:T(8,128)(2,1)S(1)} %collective-permute-done.24.refs_7_), channel_id=1, source_target_pairs={{0,1},{1,0},{2,3},{3,2},{4,5},{5,4},{6,7},{7,6},{8,9},{9,8},{10,11... | collective-permute-start | bytes 1572872 | tf_op jit(solution)/shard_map/ppermute | solution.py:59
  119.8 12.0 %collective-permute-start.25 = (bf16[256,768]{1,0:T(8,128)(2,1)S(1)}, bf16[256,768]{1,0:T(8,128)(2,1)S(1)}, u32[]{:S(2)}, u32[]{:S(2)}) collective-permute-start(bf16[256,768]{1,0:T(8,128)(2,1)S(1)} %get-tuple-element.272), channel_id=1, source_target_pairs={{0,2},{1,3},{2,0},{3,1},{4,6},{5,7},{6,4},{7,5},{8,10},{9,11},{10,... | collective-permute-start | bytes 1179656 | tf_op jit(solution)/shard_map/ppermute | solution.py:59
  120.5 18.8 %collective-permute-start.26 = (bf16[256,768]{1,0:T(8,128)(2,1)S(1)}, bf16[256,768]{1,0:T(8,128)(2,1)S(1)}, u32[]{:S(2)}, u32[]{:S(2)}) collective-permute-start(bf16[256,768]{1,0:T(8,128)(2,1)S(1)} %get-tuple-element.274), channel_id=1, source_target_pairs={{0,3},{1,2},{2,1},{3,0},{4,7},{5,6},{6,5},{7,4},{8,11},{9,10},{10,... | collective-permute-start | bytes 1179656 | tf_op jit(solution)/shard_map/ppermute | solution.py:59
  121.6 17.6 %collective-permute-start.28 = (bf16[4,256,128]{2,1,0:T(8,128)(2,1)S(1)}, bf16[4,256,128]{2,1,0:T(8,128)(2,1)S(1)}, u32[]{:S(2)}, u32[]{:S(2)}) collective-permute-start(bf16[4,256,128]{2,1,0:T(8,128)(2,1)S(1)} %back_quad.1), channel_id=1, source_target_pairs={{0,16},{4,20},{8,24},{12,28},{16,0},{20,4},{24,8},{28,12},{1,17},{... | collective-permute-start | bytes 786440 | tf_op jit(solution)/shard_map/ppermute | solution.py:59
  140.1 6.1 %collective-permute-start.31 = (bf16[256,768]{1,0:T(8,128)(2,1)S(1)}, bf16[256,768]{1,0:T(8,128)(2,1)S(1)}, u32[]{:S(2)}, u32[]{:S(2)}) collective-permute-start(bf16[256,768]{1,0:T(8,128)(2,1)S(1)} %get-tuple-element.286), channel_id=1, source_target_pairs={{0,1},{1,0},{2,3},{3,2},{4,5},{5,4},{6,7},{7,6},{8,9},{9,8},{10,11... | collective-permute-start | bytes 1179656 | tf_op jit(solution)/shard_map/ppermute | solution.py:59
  140.4 8.4 %collective-permute-start.30 = (bf16[4,256,128]{2,1,0:T(8,128)(2,1)S(1)}, bf16[4,256,128]{2,1,0:T(8,128)(2,1)S(1)}, u32[]{:S(2)}, u32[]{:S(2)}) collective-permute-start(bf16[4,256,128]{2,1,0:T(8,128)(2,1)S(1)} %get-tuple-element.277), channel_id=1, source_target_pairs={{0,4},{4,0},{8,12},{12,8},{16,20},{20,16},{24,28},{28,24},{1,5},{5... | collective-permute-start | bytes 786440 | tf_op jit(solution)/shard_map/ppermute | solution.py:59
  142.6 10.7 %collective-permute-start.33 = (bf16[2,704,128]{2,1,0:T(8,128)(2,1)S(1)}, bf16[2,704,128]{2,1,0:T(8,128)(2,1)S(1)}, u32[]{:S(2)}, u32[]{:S(2)}) collective-permute-start(bf16[2,704,128]{2,1,0:T(8,128)(2,1)S(1)} %get-tuple-element.302), channel_id=1, source_target_pairs={{0,8},{4,12},{8,0},{12,4},{16,24},{20,28},{24,16},{28,20},{1,9},{5... | collective-permute-start | bytes 1081352 | tf_op jit(solution)/shard_map/ppermute | solution.py:59
  150.6 32.0 %collective-permute-start.37 = (bf16[4,128,768]{2,1,0:T(8,128)(2,1)S(1)}, bf16[4,128,768]{2,1,0:T(8,128)(2,1)S(1)}, u32[]{:S(2)}, u32[]{:S(2)}) collective-permute-start(bf16[4,128,768]{2,1,0:T(8,128)(2,1)S(1)} %get-tuple-element.317), channel_id=1, source_target_pairs={{0,4},{4,0},{8,12},{12,8},{16,20},{20,16},{24,28},{28,24},{1,5},{5... | collective-permute-start | bytes 2359304 | tf_op jit(solution)/shard_map/ppermute | solution.py:59
  152.1 9.1 %collective-permute-start.34 = (bf16[256,512]{1,0:T(8,128)(2,1)S(1)}, bf16[256,512]{1,0:T(8,128)(2,1)S(1)}, u32[]{:S(2)}, u32[]{:S(2)}) collective-permute-start(bf16[256,512]{1,0:T(8,128)(2,1)S(1)} %get-tuple-element.308), channel_id=1, source_target_pairs={{0,2},{1,3},{2,0},{3,1},{4,6},{5,7},{6,4},{7,5},{8,10},{9,11},{10,... | collective-permute-start | bytes 786440 | tf_op jit(solution)/shard_map/ppermute | solution.py:59
  152.7 15.2 %collective-permute-start.29 = (bf16[2,704,128]{2,1,0:T(8,128)(2,1)S(1)}, bf16[2,704,128]{2,1,0:T(8,128)(2,1)S(1)}, u32[]{:S(2)}, u32[]{:S(2)}) collective-permute-start(bf16[2,704,128]{2,1,0:T(8,128)(2,1)S(1)} %get-tuple-element.284), channel_id=1, source_target_pairs={{0,8},{4,12},{8,0},{12,4},{16,24},{20,28},{24,16},{28,20},{1,9},{5... | collective-permute-start | bytes 1081352 | tf_op jit(solution)/shard_map/ppermute | solution.py:59
  153.4 12.7 %collective-permute-start.35 = (bf16[256,512]{1,0:T(8,128)(2,1)S(1)}, bf16[256,512]{1,0:T(8,128)(2,1)S(1)}, u32[]{:S(2)}, u32[]{:S(2)}) collective-permute-start(bf16[256,512]{1,0:T(8,128)(2,1)S(1)} %get-tuple-element.310), channel_id=1, source_target_pairs={{0,3},{1,2},{2,1},{3,0},{4,7},{5,6},{6,5},{7,4},{8,11},{9,10},{10,... | collective-permute-start | bytes 786440 | tf_op jit(solution)/shard_map/ppermute | solution.py:59
  154.4 24.4 %collective-permute-start.39 = (bf16[2,704,128]{2,1,0:T(8,128)(2,1)S(1)}, bf16[2,704,128]{2,1,0:T(8,128)(2,1)S(1)}, u32[]{:S(2)}, u32[]{:S(2)}) collective-permute-start(bf16[2,704,128]{2,1,0:T(8,128)(2,1)S(1)} %get-tuple-element.320), channel_id=1, source_target_pairs={{0,4},{4,0},{8,12},{12,8},{16,20},{20,16},{24,28},{28,24},{1,5},{5... | collective-permute-start | bytes 1081352 | tf_op jit(solution)/shard_map/ppermute | solution.py:59
  161.2 10.6 %collective-permute-start.40 = (bf16[1,704,128]{2,1,0:T(8,128)(2,1)S(1)}, bf16[1,704,128]{2,1,0:T(8,128)(2,1)S(1)}, u32[]{:S(2)}, u32[]{:S(2)}) collective-permute-start(bf16[1,704,128]{2,1,0:T(8,128)(2,1)S(1)} %get-tuple-element.321), channel_id=1, source_target_pairs={{0,16},{4,20},{8,24},{12,28},{16,0},{20,4},{24,8},{28,12},{1,17},{... | collective-permute-start | bytes 540680 | tf_op jit(solution)/shard_map/ppermute | solution.py:59
  168.6 13.2 %collective-permute-start.38 = (bf16[1,704,128]{2,1,0:T(8,128)(2,1)S(1)}, bf16[1,704,128]{2,1,0:T(8,128)(2,1)S(1)}, u32[]{:S(2)}, u32[]{:S(2)}) collective-permute-start(bf16[1,704,128]{2,1,0:T(8,128)(2,1)S(1)} %get-tuple-element.318), channel_id=1, source_target_pairs={{0,16},{4,20},{8,24},{12,28},{16,0},{20,4},{24,8},{28,12},{1,17},{... | collective-permute-start | bytes 540680 | tf_op jit(solution)/shard_map/ppermute | solution.py:59
  170.9 16.5 %collective-permute-start.36 = (bf16[256,1024]{1,0:T(8,128)(2,1)S(1)}, bf16[256,1024]{1,0:T(8,128)(2,1)S(1)}, u32[]{:S(2)}, u32[]{:S(2)}) collective-permute-start(bf16[256,1024]{1,0:T(8,128)(2,1)S(1)} %down_add.1), channel_id=1, source_target_pairs={{0,2},{1,3},{2,0},{3,1},{4,6},{5,7},{6,4},{7,5},{8,10},{9,11},{10,... | collective-permute-start | bytes 1572872 | tf_op jit(solution)/shard_map/ppermute | solution.py:59
  171.8 25.4 %collective-permute-start.41 = (bf16[4,128,512]{2,1,0:T(8,128)(2,1)S(1)}, bf16[4,128,512]{2,1,0:T(8,128)(2,1)S(1)}, u32[]{:S(2)}, u32[]{:S(2)}) collective-permute-start(bf16[4,128,512]{2,1,0:T(8,128)(2,1)S(1)} %get-tuple-element.334), channel_id=1, source_target_pairs={{0,4},{4,0},{8,12},{12,8},{16,20},{20,16},{24,28},{28,24},{1,5},{5... | collective-permute-start | bytes 1572872 | tf_op jit(solution)/shard_map/ppermute | solution.py:59
  183.3 13.2 %collective-permute-start.42 = (bf16[2,128,768]{2,1,0:T(8,128)(2,1)S(1)}, bf16[2,128,768]{2,1,0:T(8,128)(2,1)S(1)}, u32[]{:S(2)}, u32[]{:S(2)}) collective-permute-start(bf16[2,128,768]{2,1,0:T(8,128)(2,1)S(1)} %get-tuple-element.335), channel_id=1, source_target_pairs={{0,8},{4,12},{8,0},{12,4},{16,24},{20,28},{24,16},{28,20},{1,9},{5... | collective-permute-start | bytes 1179656 | tf_op jit(solution)/shard_map/ppermute | solution.py:59
  184.5 10.3 %collective-permute-start.43 = (bf16[1,704,128]{2,1,0:T(8,128)(2,1)S(1)}, bf16[1,704,128]{2,1,0:T(8,128)(2,1)S(1)}, u32[]{:S(2)}, u32[]{:S(2)}) collective-permute-start(bf16[1,704,128]{2,1,0:T(8,128)(2,1)S(1)} %get-tuple-element.336), channel_id=1, source_target_pairs={{0,16},{4,20},{8,24},{12,28},{16,0},{20,4},{24,8},{28,12},{1,17},{... | collective-permute-start | bytes 540680 | tf_op jit(solution)/shard_map/ppermute | solution.py:59
  197.9 13.9 %collective-permute-start.44 = (bf16[2,128,512]{2,1,0:T(8,128)(2,1)S(1)}, bf16[2,128,512]{2,1,0:T(8,128)(2,1)S(1)}, u32[]{:S(2)}, u32[]{:S(2)}) collective-permute-start(bf16[2,128,512]{2,1,0:T(8,128)(2,1)S(1)} %get-tuple-element.345), channel_id=1, source_target_pairs={{0,8},{4,12},{8,0},{12,4},{16,24},{20,28},{24,16},{28,20},{1,9},{5... | collective-permute-start | bytes 786440 | tf_op jit(solution)/shard_map/ppermute | solution.py:59
  201.1 10.6 %collective-permute-start.45 = (bf16[1,128,768]{2,1,0:T(8,128)(2,1)S(1)}, bf16[1,128,768]{2,1,0:T(8,128)(2,1)S(1)}, u32[]{:S(2)}, u32[]{:S(2)}) collective-permute-start(bf16[1,128,768]{2,1,0:T(8,128)(2,1)S(1)} %get-tuple-element.346), channel_id=1, source_target_pairs={{0,16},{4,20},{8,24},{12,28},{16,0},{20,4},{24,8},{28,12},{1,17},{... | collective-permute-start | bytes 589832 | tf_op jit(solution)/shard_map/ppermute | solution.py:59
  212.4 6.9 %collective-permute-start.46 = (bf16[1,128,512]{2,1,0:T(8,128)(2,1)S(1)}, bf16[1,128,512]{2,1,0:T(8,128)(2,1)S(1)}, u32[]{:S(2)}, u32[]{:S(2)}) collective-permute-start(bf16[1,128,512]{2,1,0:T(8,128)(2,1)S(1)} %get-tuple-element.352), channel_id=1, source_target_pairs={{0,16},{4,20},{8,24},{12,28},{16,0},{20,4},{24,8},{28,12},{1,17},{... | collective-permute-start | bytes 393224 | tf_op jit(solution)/shard_map/ppermute | solution.py:59
  212.5 7.4 %collective-permute-start.50 = (bf16[128,768]{1,0:T(8,128)(2,1)S(1)}, bf16[128,768]{1,0:T(8,128)(2,1)S(1)}, u32[]{:S(2)}, u32[]{:S(2)}) collective-permute-start(bf16[128,768]{1,0:T(8,128)(2,1)S(1)} %d_early_sum.1.refs_1_), channel_id=1, source_target_pairs={{0,2},{1,3},{2,0},{3,1},{4,6},{5,7},{6,4},{7,5},{8,10},{9,11},{10,... | collective-permute-start | bytes 589832 | tf_op jit(solution)/shard_map/ppermute | solution.py:59
  219.3 5.0 %collective-permute-start.47 = (bf16[128,512]{1,0:T(8,128)(2,1)S(1)}, bf16[128,512]{1,0:T(8,128)(2,1)S(1)}, u32[]{:S(2)}, u32[]{:S(2)}) collective-permute-start(bf16[128,512]{1,0:T(8,128)(2,1)S(1)} %d_late_sum.1.refs_5_), channel_id=1, source_target_pairs={{0,2},{1,3},{2,0},{3,1},{4,6},{5,7},{6,4},{7,5},{8,10},{9,11},{10,... | collective-permute-start | bytes 393224 | tf_op jit(solution)/shard_map/ppermute | solution.py:59
  219.9 5.8 %collective-permute-start.49 = (bf16[128,768]{1,0:T(8,128)(2,1)S(1)}, bf16[128,768]{1,0:T(8,128)(2,1)S(1)}, u32[]{:S(2)}, u32[]{:S(2)}) collective-permute-start(bf16[128,768]{1,0:T(8,128)(2,1)S(1)} %d_early_sum.1.refs_1_), channel_id=1, source_target_pairs={{0,1},{1,0},{2,3},{3,2},{4,5},{5,4},{6,7},{7,6},{8,9},{9,8},{10,11... | collective-permute-start | bytes 589832 | tf_op jit(solution)/shard_map/ppermute | solution.py:59
  219.9 6.0 %collective-permute-start.51 = (bf16[128,768]{1,0:T(8,128)(2,1)S(1)}, bf16[128,768]{1,0:T(8,128)(2,1)S(1)}, u32[]{:S(2)}, u32[]{:S(2)}) collective-permute-start(bf16[128,768]{1,0:T(8,128)(2,1)S(1)} %collective-permute-done.50.refs_3_), channel_id=1, source_target_pairs={{0,1},{1,0},{2,3},{3,2},{4,5},{5,4},{6,7},{7,6},{8,9},{9,8},{10,11... | collective-permute-start | bytes 589832 | tf_op jit(solution)/shard_map/ppermute | solution.py:59
  (17 other events, 123.2 us)
where the time goes:
time: 233 us; the launch traced here: 229 us
  waiting for transfers between devices  100 us (43%)
  Pallas kernels  68 us (29%)
  starting transfers between devices  52.4 us (22%)
  local copies, waits for them, and re-layouts  5.12 us (2%)
    ppermute x53, waiting for transfers between devices, swap(): return lax.ppermute(array, axis, [(i, i ^ bit) for i in range(count)])  100 us
    pallas_call x42, Pallas kernels, run(): pl.pallas_call(kernel, name=name, out_shape=[shape_of(s, k) for s, k in o...  68 us
    ppermute x53, starting transfers between devices, swap(): return lax.ppermute(array, axis, [(i, i ^ bit) for i in range(count)])  52.4 us
    unnamed x24, local copies, waits for them, and re-layouts  5.12 us
  transfers between devices with their start and end apart: 53, of which 23 were waited for; matrix products, arithmetic and copies ran while one was open for 0% of the time, Pallas kernels for 24%

commit v1 on v0

--- a/solution.py
+++ b/solution.py
@@ -704,6 +704,7 @@
         [(small, F32), (small, BF), (small, BF), (small, BF), state, state],
         [forget, numbers],
         [part_2, back_0, part_1, resid, down_low, attention, update, query, w_out],
+        BRIEF,
     )
 
     def mix_weight(name, groups, arrays, columns, time=BRIEF):
@@ -763,18 +764,18 @@
         line, send, keep, numbers, forget, span, True, (back_1_, back_2_, back_3_, back_4_)
     )
     key_part, value_part = got["early"][4:6]
-    early_sum = got["early_sum"]
     *late, late_pieces = line.run(
         "late",
         late_kernel,
         [((span, 2 * quarter), BF)] * 4 + [((4, span, 2 * quarter), BF)],
         [numbers, forget],
         [after_theirs, after_mine, value, key, raw_key, cosine, sine, key_part, value_part],
+        BRIEF,
     )
     late_2, late_3 = line.swap(late[2], "tp", 2), line.swap(late[3], "tp", 3)
     late_1 = line.swap(late[1], "tp", 1)
     down_sum.go()
-    early_sum.go()
+    got["early_sum"].go()
     gate_sum.join()
     gate_sum.go()
     line.wait(late_2, late_3)
@@ -783,6 +784,7 @@
         [(more, four, 0, 2 * quarter)],
         [late_1, late[0], late_2, late_3] + [normed_rows[k] for k in (1, 0, 2, 3)],
         2 * quarter,
+        BRIEF,
     )
     late_sum.go()
     up_sum.join()
@@ -791,29 +793,30 @@
     gate_grad = gate_sum.total(F32)
     down_sum.join()
     down_sum.go()
+    up_grad = up_sum.total(F32)
+    got["early_sum"].join()
+    got["early_sum"].go()
     d_tokens = line.run(
         "d_tokens",
         tokens_kernel,
         [(small, BF)],
         [],
         [late_pieces, got["normed_grad"], resid_grad, tokens, w_mix],
+        BRIEF,
     )[0]
-    up_grad = up_sum.total(F32)
-    early_sum.join()
-    early_sum.go()
+    got["early_sum"].join()
+    got["early_sum"].go()
     out = line.run("out", out_kernel, [(small, BF)], [numbers, lengths], [down_2, downs[0], down_1, resid])[0]
     down_grad = down_sum.total(F32)
-    early_sum.join()
-    early_sum.go()
     late_sum.join()
     late_sum.go()
-    early_all = early_sum.total(BF)
+    early_all = got["early_sum"].total(BF)
     early_full = [early_all, line.swap(early_all, "tp", 1), line.swap(early_all, "tp", 2)]
     late_sum.join()
     late_sum.go()
     late_all = late_sum.total(BF)
+    late_full = [late_all, line.swap(late_all, "tp", 1), line.swap(late_all, "tp", 2)]
     early_full.append(line.swap(early_full[2], "tp", 1))
-    late_full = [late_all, line.swap(late_all, "tp", 1), line.swap(late_all, "tp", 2)]
     late_full.append(swap(late_full[2], "tp", 1))
     rows = early_full[0].shape[0]
     mix_sum, out_sum = line.run(

time: 233 us -> 235 us (level)
  transfers between devices with their start and end apart: 53 -> 53, of which waited for: 23 -> 24; matrix products, arithmetic and copies ran while one was open for 0% -> 0% of each run, Pallas kernels for 24% -> 23%
where the time goes in v1:
time: 235 us; the launch traced here: 230 us
  waiting for transfers between devices  100 us (43%)
  Pallas kernels  68 us (29%)
  starting transfers between devices  54.1 us (23%)
  local copies, waits for them, and re-layouts  5.12 us (2%)
    ppermute x53, waiting for transfers between devices, swap(): return lax.ppermute(array, axis, [(i, i ^ bit) for i in range(count)])  100 us
    pallas_call x42, Pallas kernels, run(): pl.pallas_call(kernel, name=name, out_shape=[shape_of(s, k) for s, k in o...  68 us
    ppermute x53, starting transfers between devices, swap(): return lax.ppermute(array, axis, [(i, i ^ bit) for i in range(count)])  54.1 us
    unnamed x24, local copies, waits for them, and re-layouts  5.12 us
  transfers between devices with their start and end apart: 53, of which 24 were waited for; matrix products, arithmetic and copies ran while one was open for 0% of the time, Pallas kernels for 23%

profile of v1, /device:TPU:0, one launch (start us, length us, event | category | flops | bytes accessed | tf_op | source)
XLA Modules:
  0.0 230.2 jit_solution(9393766031388026328)
XLA Ops:
  2.0 3.4 %copy-done = bf16[1024,4096]{1,0:T(8,128)(2,1)S(1)} copy-done((bf16[1024,4096]{1,0:T(8,128)(2,1)S(1)}, bf16[1024,4096]{1,0:T(8,128)(2,1)}, u32[]{:S(2)}) %copy-start) | copy-done | bytes 8388632
  7.1 3.1 %key_value.1 = (bf16[256,1024]{1,0:T(8,128)(2,1)S(1)}, f32[256,1024]{1,0:T(8,128)S(1)}, bf16[256,2048]{1,0:T(8,128)(2,1)S(1)}, bf16[256,1024]{1,0:T(8,128)(2,1)S...) custom-call(s32[3]{0:T(128)S(1)} %pad_add_fusion.numbers.refs_0_, f32[8]{0:T(128)S(1)} %copy-done.9, ...), custom_call_target="tpu_custom_call" | custom-call | flops 22000000 | bytes 1024 | tf_op jit(solution)/shard_map/key_value/pallas_call | solution.py:122
  10.2 3.0 %collective-permute-start = (bf16[4,256,128]{2,1,0:T(8,128)(2,1)S(1)}, bf16[4,256,128]{2,1,0:T(8,128)(2,1)S(1)}, u32[]{:S(2)}, u32[]{:S(2)}) collective-permute-start(bf16[4,256,128]{2,1,0:T(8,128)(2,1)S(1)} %get-tuple-element.191), channel_id=1, source_target_pairs={{0,4},{4,0},{8,12},{12,8},{16,20},{20,16},{24,28},{28,24},{1,5},{5... | collective-permute-start | bytes 786440 | tf_op jit(solution)/shard_map/ppermute | solution.py:59
  13.2 2.8 %query.1 = (f32[256,1024]{1,0:T(8,128)S(1)}, bf16[256,2048]{1,0:T(8,128)(2,1)S(1)}, f32[256,1024]{1,0:T(8,128)S(1)}, bf16[8,256,256]{2,1,0:T(8,128)(2,1)S(1)}, f...) custom-call(s32[3]{0:T(128)S(1)} %pad_add_fusion.numbers.refs_0_, s32[4]{0:T(128)S(1)} %copy-done.11, ...), custom_call_target="tpu_custom_call" | custom-call | flops 22000000 | bytes 1024 | tf_op jit(solution)/shard_map/query/pallas_call | solution.py:122
  16.1 3.5 %collective-permute-done.other = bf16[4,256,128]{2,1,0:T(8,128)(2,1)S(1)} collective-permute-done((bf16[4,256,128]{2,1,0:T(8,128)(2,1)S(1)}, bf16[4,256,128]{2,1,0:T(8,128)(2,1)S(1)}, u32[]{:S(2)}, u32[]{:S(2)}) %collective-permute-start) | collective-permute-done | bytes 262176 | tf_op jit(solution)/shard_map/ppermute | solution.py:59
  20.2 1.9 collective-permute-start.1
  23.5 4.2 %collective-permute-done.1.near = bf16[4,256,128]{2,1,0:T(8,128)(2,1)S(1)} collective-permute-done((bf16[4,256,128]{2,1,0:T(8,128)(2,1)S(1)}, bf16[4,256,128]{2,1,0:T(8,128)(2,1)S(1)}, u32[]{:S(2)}, u32[]{:S(2)}) %collective-permute-start.1) | collective-permute-done | bytes 262176 | tf_op jit(solution)/shard_map/ppermute | solution.py:59
  28.5 2.6 %collective-permute-start.4 = (bf16[4,256,128]{2,1,0:T(8,128)(2,1)S(1)}, bf16[4,256,128]{2,1,0:T(8,128)(2,1)S(1)}, u32[]{:S(2)}, u32[]{:S(2)}) collective-permute-start(bf16[4,256,128]{2,1,0:T(8,128)(2,1)S(1)} %fore_quad.1), channel_id=1, source_target_pairs={{0,16},{4,20},{8,24},{12,28},{16,0},{20,4},{24,8},{28,12},{1,17},{... | collective-permute-start | bytes 786440 | tf_op jit(solution)/shard_map/ppermute | solution.py:59
  32.5 2.7 %collective-permute-done.2.rows_2.refs_4_ = bf16[256,1024]{1,0:T(8,128)(2,1)S(1)} collective-permute-done((bf16[256,1024]{1,0:T(8,128)(2,1)S(1)}, bf16[256,1024]{1,0:T(8,128)(2,1)S(1)}, u32[]{:S(2)}, u32[]{:S(2)}) %collective-permute-start.2) | collective-permute-done | bytes 524320 | tf_op jit(solution)/shard_map/ppermute | solution.py:59
  35.3 8.5 %collective-permute-done.4.far = bf16[4,256,128]{2,1,0:T(8,128)(2,1)S(1)} collective-permute-done((bf16[4,256,128]{2,1,0:T(8,128)(2,1)S(1)}, bf16[4,256,128]{2,1,0:T(8,128)(2,1)S(1)}, u32[]{:S(2)}, u32[]{:S(2)}) %collective-permute-start.4) | collective-permute-done | bytes 262176 | tf_op jit(solution)/shard_map/ppermute | solution.py:59
  46.1 7.2 %collective-permute-done.5.theirs = bf16[4,256,128]{2,1,0:T(8,128)(2,1)S(1)} collective-permute-done((bf16[4,256,128]{2,1,0:T(8,128)(2,1)S(1)}, bf16[4,256,128]{2,1,0:T(8,128)(2,1)S(1)}, u32[]{:S(2)}, u32[]{:S(2)}) %collective-permute-start.5) | collective-permute-done | bytes 262176 | tf_op jit(solution)/shard_map/ppermute | solution.py:59
  53.4 2.0 mix.1
  57.8 1.8 hidden_grad.1
  59.7 3.6 %ffn_near.1 = (bf16[512,704]{1,0:T(8,128)(2,1)S(1)}, bf16[512,704]{1,0:T(8,128)(2,1)S(1)}, bf16[512,704]{1,0:T(8,128)(2,1)S(1)}, bf16[256,1024]{1,0:T(8,128)(2,1)S(1)}, bf16[256,1024]{1,0:T(8,128)(2,1)S(1)}) custom-call(bf16[256,1024]{1,0:T(8,128)(2,1)S(1)} %collective-permute-done.8.rows_1.refs_3_, bf16[256,1024]{1,0:T(8,128)(2,1)S(1)} %get-tuple-element.209.rows_0.refs_2_, ...), custom_call_target="tpu_custom_call" | custom-call | flops 22000000 | bytes 1024 | tf_op jit(solution)/shard_map/ffn_near/pallas_call | solution.py:122
  63.3 7.0 %collective-permute-done.12.rows_0.refs_4_ = bf16[256,1024]{1,0:T(8,128)(2,1)S(1)} collective-permute-done((bf16[256,1024]{1,0:T(8,128)(2,1)S(1)}, bf16[256,1024]{1,0:T(8,128)(2,1)S(1)}, u32[]{:S(2)}, u32[]{:S(2)}) %collective-permute-start.12) | collective-permute-done | bytes 524320 | tf_op jit(solution)/shard_map/ppermute | solution.py:59
  70.3 1.9 collective-permute-done.13.rows_1.refs_5_
  72.2 3.9 %ffn_far.1 = (bf16[512,704]{1,0:T(8,128)(2,1)S(1)}, bf16[512,704]{1,0:T(8,128)(2,1)S(1)}, bf16[512,704]{1,0:T(8,128)(2,1)S(1)}, bf16[256,1024]{1,0:T(8,128)(2,1)S(1)}, bf16[256,1024]{1,0:T(8,128)(2,1)S(1)}) custom-call(bf16[256,1024]{1,0:T(8,128)(2,1)S(1)} %collective-permute-done.13.rows_1.refs_5_, ...), custom_call_target="tpu_custom_call" | custom-call | flops 22000000 | bytes 1024 | tf_op jit(solution)/shard_map/ffn_far/pallas_call | solution.py:122
  76.7 2.2 d_gate.1
  82.1 2.2 d_down.1
  85.1 1.8 down.1
  87.5 2.2 d_up.1
  89.7 4.6 %collective-permute-done.17.part_0 = bf16[256,1024]{1,0:T(8,128)(2,1)S(1)} collective-permute-done((bf16[256,1024]{1,0:T(8,128)(2,1)S(1)}, bf16[256,1024]{1,0:T(8,128)(2,1)S(1)}, u32[]{:S(2)}, u32[]{:S(2)}) %collective-permute-start.17) | collective-permute-done | bytes 524320 | tf_op jit(solution)/shard_map/ppermute | solution.py:59
  94.3 2.6 %resid.1 = (f32[256,1024]{1,0:T(8,128)S(1)}, bf16[256,1024]{1,0:T(8,128)(2,1)S(1)}, bf16[256,1024]{1,0:T(8,128)(2,1)S(1)}, bf16[256,1024]{1,0:T(8,128)(2,1)S(1)}...) custom-call(f32[8]{0:T(128)S(1)} %copy-done.10, s32[3]{0:T(128)S(1)} %pad_add_fusion.numbers.refs_0_, ...), custom_call_target="tpu_custom_call" | custom-call | flops 22000000 | bytes 1024 | tf_op jit(solution)/shard_map/resid/pallas_call | solution.py:122
  99.0 12.4 %early.1 = (bf16[256,768]{1,0:T(8,128)(2,1)S(1)}, bf16[256,768]{1,0:T(8,128)(2,1)S(1)}, bf16[256,768]{1,0:T(8,128)(2,1)S(1)}, bf16[256,768]{1,0:T(8,128)(2,1)S(1...) custom-call(s32[3]{0:T(128)S(1)} %pad_add_fusion.numbers.refs_0_, ...), custom_call_target="tpu_custom_call" | custom-call | flops 22000000 | bytes 1024 | tf_op jit(solution)/shard_map/early/pallas_call | solution.py:122
  114.5 4.5 %collective-permute-done.23.near = bf16[4,256,128]{2,1,0:T(8,128)(2,1)S(1)} collective-permute-done((bf16[4,256,128]{2,1,0:T(8,128)(2,1)S(1)}, bf16[4,256,128]{2,1,0:T(8,128)(2,1)S(1)}, u32[]{:S(2)}, u32[]{:S(2)}) %collective-permute-start.23) | collective-permute-done | bytes 262176 | tf_op jit(solution)/shard_map/ppermute | solution.py:59
  121.6 2.3 %collective-permute-start.28 = (bf16[4,256,128]{2,1,0:T(8,128)(2,1)S(1)}, bf16[4,256,128]{2,1,0:T(8,128)(2,1)S(1)}, u32[]{:S(2)}, u32[]{:S(2)}) collective-permute-start(bf16[4,256,128]{2,1,0:T(8,128)(2,1)S(1)} %back_quad.1), channel_id=1, source_target_pairs={{0,16},{4,20},{8,24},{12,28},{16,0},{20,4},{24,8},{28,12},{1,17},{... | collective-permute-start | bytes 786440 | tf_op jit(solution)/shard_map/ppermute | solution.py:59
  123.9 7.8 %collective-permute-done.25.refs_3_ = bf16[256,768]{1,0:T(8,128)(2,1)S(1)} collective-permute-done((bf16[256,768]{1,0:T(8,128)(2,1)S(1)}, bf16[256,768]{1,0:T(8,128)(2,1)S(1)}, u32[]{:S(2)}, u32[]{:S(2)}) %collective-permute-start.25) | collective-permute-done | bytes 393248 | tf_op jit(solution)/shard_map/ppermute | solution.py:59
  131.7 7.5 %collective-permute-done.26.refs_4_ = bf16[256,768]{1,0:T(8,128)(2,1)S(1)} collective-permute-done((bf16[256,768]{1,0:T(8,128)(2,1)S(1)}, bf16[256,768]{1,0:T(8,128)(2,1)S(1)}, u32[]{:S(2)}, u32[]{:S(2)}) %collective-permute-start.26) | collective-permute-done | bytes 393248 | tf_op jit(solution)/shard_map/ppermute | solution.py:59
  146.2 2.5 %d_early.1 = (bf16[4,128,768]{2,1,0:T(8,128)(2,1)S(1)}, bf16[4,128,768]{2,1,0:T(8,128)(2,1)S(1)}) custom-call(s32[3]{0:T(128)S(1)} %pad_add_fusion.numbers.refs_0_, bf16[256,768]{1,0:T(8,128)(2,1)S(1)} %collective-permute-done.31.refs_1_, bf16[256,768]{1,0:T(8,128)(2,1)S(1)} %get-tuple-element.258.refs_2_, ...), custom_call_target="tpu_custom_call" | custom-call | flops 22000000 | bytes 1024 | tf_op jit(solution)/shard_map/d_early/pallas_call | solution.py:122
  148.8 1.7 late.1
  150.6 1.6 collective-permute-start.37
  156.0 5.2 %collective-permute-done.34.refs_3_ = bf16[256,512]{1,0:T(8,128)(2,1)S(1)} collective-permute-done((bf16[256,512]{1,0:T(8,128)(2,1)S(1)}, bf16[256,512]{1,0:T(8,128)(2,1)S(1)}, u32[]{:S(2)}, u32[]{:S(2)}) %collective-permute-start.34) | collective-permute-done | bytes 262176 | tf_op jit(solution)/shard_map/ppermute | solution.py:59
  161.2 2.3 %collective-permute-start.40 = (bf16[1,704,128]{2,1,0:T(8,128)(2,1)S(1)}, bf16[1,704,128]{2,1,0:T(8,128)(2,1)S(1)}, u32[]{:S(2)}, u32[]{:S(2)}) collective-permute-start(bf16[1,704,128]{2,1,0:T(8,128)(2,1)S(1)} %get-tuple-element.320), channel_id=1, source_target_pairs={{0,16},{4,20},{8,24},{12,28},{16,0},{20,4},{24,8},{28,12},{1,17},{... | collective-permute-start | bytes 540680 | tf_op jit(solution)/shard_map/ppermute | solution.py:59
  163.6 2.5 %collective-permute-done.35.refs_4_ = bf16[256,512]{1,0:T(8,128)(2,1)S(1)} collective-permute-done((bf16[256,512]{1,0:T(8,128)(2,1)S(1)}, bf16[256,512]{1,0:T(8,128)(2,1)S(1)}, u32[]{:S(2)}, u32[]{:S(2)}) %collective-permute-start.35) | collective-permute-done | bytes 262176 | tf_op jit(solution)/shard_map/ppermute | solution.py:59
  166.1 1.8 d_late.1
  168.6 2.4 %collective-permute-start.38 = (bf16[1,704,128]{2,1,0:T(8,128)(2,1)S(1)}, bf16[1,704,128]{2,1,0:T(8,128)(2,1)S(1)}, u32[]{:S(2)}, u32[]{:S(2)}) collective-permute-start(bf16[1,704,128]{2,1,0:T(8,128)(2,1)S(1)} %get-tuple-element.318), channel_id=1, source_target_pairs={{0,16},{4,20},{8,24},{12,28},{16,0},{20,4},{24,8},{28,12},{1,17},{... | collective-permute-start | bytes 540680 | tf_op jit(solution)/shard_map/ppermute | solution.py:59
  173.6 5.2 %collective-permute-done.39.other = bf16[2,704,128]{2,1,0:T(8,128)(2,1)S(1)} collective-permute-done((bf16[2,704,128]{2,1,0:T(8,128)(2,1)S(1)}, bf16[2,704,128]{2,1,0:T(8,128)(2,1)S(1)}, u32[]{:S(2)}, u32[]{:S(2)}) %collective-permute-start.39) | collective-permute-done | bytes 360480 | tf_op jit(solution)/shard_map/ppermute | solution.py:59
  182.4 3.4 %collective-permute-start.43 = (bf16[1,704,128]{2,1,0:T(8,128)(2,1)S(1)}, bf16[1,704,128]{2,1,0:T(8,128)(2,1)S(1)}, u32[]{:S(2)}, u32[]{:S(2)}) collective-permute-start(bf16[1,704,128]{2,1,0:T(8,128)(2,1)S(1)} %get-tuple-element.339), channel_id=1, source_target_pairs={{0,16},{4,20},{8,24},{12,28},{16,0},{20,4},{24,8},{28,12},{1,17},{... | collective-permute-start | bytes 540680 | tf_op jit(solution)/shard_map/ppermute | solution.py:59
  185.7 2.3 %d_tokens.1 = bf16[256,1024]{1,0:T(8,128)(2,1)} custom-call(bf16[4,256,512]{2,1,0:T(8,128)(2,1)S(1)} %get-tuple-element.333.pieces, f32[256,1024]{1,0:T(8,128)S(1)} %normed_grad.1.early, f32[256,1024]{1,0:T(8,128)S(1)} %get-tuple-element.249.resid_grad, bf16[256,1024]{1,0:T(8,128)(2,1)S(1)} %bitcast.21, bf16[1024,4096]{1,0:T(8,128)(2,1)S(1)} %copy-done.1), custom_call_target="tpu_custom_call" | custom-call | flops 22000000 | bytes 1024 | tf_op jit(solution)/shard_map/d_tokens/pallas_call | solution.py:122
  188.1 8.5 %collective-permute-done.41.other = bf16[2,128,768]{2,1,0:T(8,128)(2,1)S(1)} collective-permute-done((bf16[2,128,768]{2,1,0:T(8,128)(2,1)S(1)}, bf16[2,128,768]{2,1,0:T(8,128)(2,1)S(1)}, u32[]{:S(2)}, u32[]{:S(2)}) %collective-permute-start.41) | collective-permute-done | bytes 393248 | tf_op jit(solution)/shard_map/ppermute | solution.py:59
  197.2 1.6 out.1
  200.4 4.0 %collective-permute-start.45 = (bf16[1,128,768]{2,1,0:T(8,128)(2,1)S(1)}, bf16[1,128,768]{2,1,0:T(8,128)(2,1)S(1)}, u32[]{:S(2)}, u32[]{:S(2)}) collective-permute-start(bf16[1,128,768]{2,1,0:T(8,128)(2,1)S(1)} %get-tuple-element.346), channel_id=1, source_target_pairs={{0,16},{4,20},{8,24},{12,28},{16,0},{20,4},{24,8},{28,12},{1,17},{... | collective-permute-start | bytes 589832 | tf_op jit(solution)/shard_map/ppermute | solution.py:59
  204.4 5.0 %collective-permute-done.45.other = bf16[1,128,768]{2,1,0:T(8,128)(2,1)S(1)} collective-permute-done((bf16[1,128,768]{2,1,0:T(8,128)(2,1)S(1)}, bf16[1,128,768]{2,1,0:T(8,128)(2,1)S(1)}, u32[]{:S(2)}, u32[]{:S(2)}) %collective-permute-start.45) | collective-permute-done | bytes 196640 | tf_op jit(solution)/shard_map/ppermute | solution.py:59
  209.5 2.1 collective-permute-done.44.other
  212.2 2.1 collective-permute-start.46
  214.9 6.0 %collective-permute-done.46.other = bf16[1,128,512]{2,1,0:T(8,128)(2,1)S(1)} collective-permute-done((bf16[1,128,512]{2,1,0:T(8,128)(2,1)S(1)}, bf16[1,128,512]{2,1,0:T(8,128)(2,1)S(1)}, u32[]{:S(2)}, u32[]{:S(2)}) %collective-permute-start.46) | collective-permute-done | bytes 131104 | tf_op jit(solution)/shard_map/ppermute | solution.py:59
  222.0 3.9 %collective-permute-done.47.refs_7_ = bf16[128,512]{1,0:T(8,128)(2,1)S(1)} collective-permute-done((bf16[128,512]{1,0:T(8,128)(2,1)S(1)}, bf16[128,512]{1,0:T(8,128)(2,1)S(1)}, u32[]{:S(2)}, u32[]{:S(2)}) %collective-permute-start.47) | collective-permute-done | bytes 131104 | tf_op jit(solution)/shard_map/ppermute | solution.py:59
  227.4 2.6 %collect.1 = (f32[128,4096]{1,0:T(8,128)}, f32[128,1024]{1,0:T(8,128)}) custom-call(s32[3]{0:T(128)S(1)} %pad_add_fusion.numbers.refs_0_, bf16[128,512]{1,0:T(8,128)(2,1)S(1)} %collective-permute-done.48.refs_0_, bf16[128,768]{1,0:T(8,128)(2,1)S(1)} %d_early_sum.1.refs_1_, bf16[128,768]{1,0:T(8,128)(2,1)S(1)} %collective-permute-done.49.refs_2_, ...), custom_call_target="tpu_custom_call" | custom-call | flops 22000000 | bytes 1024 | tf_op jit(solution)/shard_map/collect/pallas_call | solution.py:122
  (127 shorter events, 49.0 us)
Async XLA Ops:
  10.2 9.3 %collective-permute-start = (bf16[4,256,128]{2,1,0:T(8,128)(2,1)S(1)}, bf16[4,256,128]{2,1,0:T(8,128)(2,1)S(1)}, u32[]{:S(2)}, u32[]{:S(2)}) collective-permute-start(bf16[4,256,128]{2,1,0:T(8,128)(2,1)S(1)} %get-tuple-element.191), channel_id=1, source_target_pairs={{0,4},{4,0},{8,12},{12,8},{16,20},{20,16},{24,28},{28,24},{1,5},{5... | collective-permute-start | bytes 786440 | tf_op jit(solution)/shard_map/ppermute | solution.py:59
  20.2 7.6 %collective-permute-start.1 = (bf16[4,256,128]{2,1,0:T(8,128)(2,1)S(1)}, bf16[4,256,128]{2,1,0:T(8,128)(2,1)S(1)}, u32[]{:S(2)}, u32[]{:S(2)}) collective-permute-start(bf16[4,256,128]{2,1,0:T(8,128)(2,1)S(1)} %fore_pair.1.pair), channel_id=1, source_target_pairs={{0,8},{4,12},{8,0},{12,4},{16,24},{20,28},{24,16},{28,20},{1,9},{5... | collective-permute-start | bytes 786440 | tf_op jit(solution)/shard_map/ppermute | solution.py:59
  22.1 13.2 %collective-permute-start.2 = (bf16[256,1024]{1,0:T(8,128)(2,1)S(1)}, bf16[256,1024]{1,0:T(8,128)(2,1)S(1)}, u32[]{:S(2)}, u32[]{:S(2)}) collective-permute-start(bf16[256,1024]{1,0:T(8,128)(2,1)S(1)} %get-tuple-element.210.rows_0.refs_2_.down_low), channel_id=1, source_target_pairs={{0,2},{1,3},{2,0},{3,1},{4,6},{5,7},{6,4},{7,5},{8,10},{9,11},{10,... | collective-permute-start | bytes 1572872 | tf_op jit(solution)/shard_map/ppermute | solution.py:59
  28.4 6.9 %collective-permute-start.3 = (bf16[256,1024]{1,0:T(8,128)(2,1)S(1)}, bf16[256,1024]{1,0:T(8,128)(2,1)S(1)}, u32[]{:S(2)}, u32[]{:S(2)}) collective-permute-start(bf16[256,1024]{1,0:T(8,128)(2,1)S(1)} %get-tuple-element.210.rows_0.refs_2_.down_low), channel_id=1, source_target_pairs={{0,1},{1,0},{2,3},{3,2},{4,5},{5,4},{6,7},{7,6},{8,9},{9,8},{10,11... | collective-permute-start | bytes 1572872 | tf_op jit(solution)/shard_map/ppermute | solution.py:59
  28.5 15.2 %collective-permute-start.4 = (bf16[4,256,128]{2,1,0:T(8,128)(2,1)S(1)}, bf16[4,256,128]{2,1,0:T(8,128)(2,1)S(1)}, u32[]{:S(2)}, u32[]{:S(2)}) collective-permute-start(bf16[4,256,128]{2,1,0:T(8,128)(2,1)S(1)} %fore_quad.1), channel_id=1, source_target_pairs={{0,16},{4,20},{8,24},{12,28},{16,0},{20,4},{24,8},{28,12},{1,17},{... | collective-permute-start | bytes 786440 | tf_op jit(solution)/shard_map/ppermute | solution.py:59
  31.0 22.3 %collective-permute-start.7 = (bf16[256,1024]{1,0:T(8,128)(2,1)S(1)}, bf16[256,1024]{1,0:T(8,128)(2,1)S(1)}, u32[]{:S(2)}, u32[]{:S(2)}) collective-permute-start(bf16[256,1024]{1,0:T(8,128)(2,1)S(1)} %get-tuple-element.213.normed.refs_10_.refs_6_), channel_id=1, source_target_pairs={{0,2},{1,3},{2,0},{3,1},{4,6},{5,7},{6,4},{7,5},{8,10},{9,11},{10,... | collective-permute-start | bytes 1572872 | tf_op jit(solution)/shard_map/ppermute | solution.py:59
  44.5 8.8 %collective-permute-start.6 = (bf16[256,1024]{1,0:T(8,128)(2,1)S(1)}, bf16[256,1024]{1,0:T(8,128)(2,1)S(1)}, u32[]{:S(2)}, u32[]{:S(2)}) collective-permute-start(bf16[256,1024]{1,0:T(8,128)(2,1)S(1)} %collective-permute-done.2.rows_2.refs_4_), channel_id=1, source_target_pairs={{0,1},{1,0},{2,3},{3,2},{4,5},{5,4},{6,7},{7,6},{8,9},{9,8},{10,11... | collective-permute-start | bytes 1572872 | tf_op jit(solution)/shard_map/ppermute | solution.py:59
  44.6 8.7 %collective-permute-start.5 = (bf16[4,256,128]{2,1,0:T(8,128)(2,1)S(1)}, bf16[4,256,128]{2,1,0:T(8,128)(2,1)S(1)}, u32[]{:S(2)}, u32[]{:S(2)}) collective-permute-start(bf16[4,256,128]{2,1,0:T(8,128)(2,1)S(1)} %get-tuple-element.198), channel_id=1, source_target_pairs={{0,4},{4,0},{8,12},{12,8},{16,20},{20,16},{24,28},{28,24},{1,5},{5... | collective-permute-start | bytes 786440 | tf_op jit(solution)/shard_map/ppermute | solution.py:59
  55.3 4.3 %collective-permute-start.8 = (bf16[256,1024]{1,0:T(8,128)(2,1)S(1)}, bf16[256,1024]{1,0:T(8,128)(2,1)S(1)}, u32[]{:S(2)}, u32[]{:S(2)}) collective-permute-start(bf16[256,1024]{1,0:T(8,128)(2,1)S(1)} %get-tuple-element.209.rows_0.refs_2_), channel_id=1, source_target_pairs={{0,1},{1,0},{2,3},{3,2},{4,5},{5,4},{6,7},{7,6},{8,9},{9,8},{10,11... | collective-permute-start | bytes 1572872 | tf_op jit(solution)/shard_map/ppermute | solution.py:59
  55.4 4.3 %collective-permute-start.9 = (bf16[256,1024]{1,0:T(8,128)(2,1)S(1)}, bf16[256,1024]{1,0:T(8,128)(2,1)S(1)}, u32[]{:S(2)}, u32[]{:S(2)}) collective-permute-start(bf16[256,1024]{1,0:T(8,128)(2,1)S(1)} %get-tuple-element.213.normed.refs_10_.refs_6_), channel_id=1, source_target_pairs={{0,1},{1,0},{2,3},{3,2},{4,5},{5,4},{6,7},{7,6},{8,9},{9,8},{10,11... | collective-permute-start | bytes 1572872 | tf_op jit(solution)/shard_map/ppermute | solution.py:59
  55.9 3.8 %collective-permute-start.10 = (bf16[256,1024]{1,0:T(8,128)(2,1)S(1)}, bf16[256,1024]{1,0:T(8,128)(2,1)S(1)}, u32[]{:S(2)}, u32[]{:S(2)}) collective-permute-start(bf16[256,1024]{1,0:T(8,128)(2,1)S(1)} %collective-permute-done.7.refs_11_.refs_7_), channel_id=1, source_target_pairs={{0,1},{1,0},{2,3},{3,2},{4,5},{5,4},{6,7},{7,6},{8,9},{9,8},{10,11... | collective-permute-start | bytes 1572872 | tf_op jit(solution)/shard_map/ppermute | solution.py:59
  56.4 13.9 %collective-permute-start.12 = (bf16[256,1024]{1,0:T(8,128)(2,1)S(1)}, bf16[256,1024]{1,0:T(8,128)(2,1)S(1)}, u32[]{:S(2)}, u32[]{:S(2)}) collective-permute-start(bf16[256,1024]{1,0:T(8,128)(2,1)S(1)} %get-tuple-element.209.rows_0.refs_2_), channel_id=1, source_target_pairs={{0,2},{1,3},{2,0},{3,1},{4,6},{5,7},{6,4},{7,5},{8,10},{9,11},{10,... | collective-permute-start | bytes 1572872 | tf_op jit(solution)/shard_map/ppermute | solution.py:59
  76.1 4.3 %collective-permute-start.14 = (bf16[256,1024]{1,0:T(8,128)(2,1)S(1)}, bf16[256,1024]{1,0:T(8,128)(2,1)S(1)}, u32[]{:S(2)}, u32[]{:S(2)}) collective-permute-start(bf16[256,1024]{1,0:T(8,128)(2,1)S(1)} %get-tuple-element.224), channel_id=1, source_target_pairs={{0,1},{1,0},{2,3},{3,2},{4,5},{5,4},{6,7},{7,6},{8,9},{9,8},{10,11... | collective-permute-start | bytes 1572872 | tf_op jit(solution)/shard_map/ppermute | solution.py:59
  76.3 4.1 %collective-permute-start.15 = (bf16[256,1024]{1,0:T(8,128)(2,1)S(1)}, bf16[256,1024]{1,0:T(8,128)(2,1)S(1)}, u32[]{:S(2)}, u32[]{:S(2)}) collective-permute-start(bf16[256,1024]{1,0:T(8,128)(2,1)S(1)} %get-tuple-element.231), channel_id=1, source_target_pairs={{0,1},{1,0},{2,3},{3,2},{4,5},{5,4},{6,7},{7,6},{8,9},{9,8},{10,11... | collective-permute-start | bytes 1572872 | tf_op jit(solution)/shard_map/ppermute | solution.py:59
  78.9 18.7 %collective-permute-start.18 = (bf16[4,704,128]{2,1,0:T(8,128)(2,1)S(1)}, bf16[4,704,128]{2,1,0:T(8,128)(2,1)S(1)}, u32[]{:S(2)}, u32[]{:S(2)}) collective-permute-start(bf16[4,704,128]{2,1,0:T(8,128)(2,1)S(1)} %get-tuple-element.251), channel_id=1, source_target_pairs={{0,4},{4,0},{8,12},{12,8},{16,20},{20,16},{24,28},{28,24},{1,5},{5... | collective-permute-start | bytes 2162696 | tf_op jit(solution)/shard_map/ppermute | solution.py:59
  80.5 13.8 %collective-permute-start.17 = (bf16[256,1024]{1,0:T(8,128)(2,1)S(1)}, bf16[256,1024]{1,0:T(8,128)(2,1)S(1)}, u32[]{:S(2)}, u32[]{:S(2)}) collective-permute-start(bf16[256,1024]{1,0:T(8,128)(2,1)S(1)} %ffn_add.1), channel_id=1, source_target_pairs={{0,2},{1,3},{2,0},{3,1},{4,6},{5,7},{6,4},{7,5},{8,10},{9,11},{10,... | collective-permute-start | bytes 1572872 | tf_op jit(solution)/shard_map/ppermute | solution.py:59
  84.3 27.2 %collective-permute-start.20 = (bf16[4,704,128]{2,1,0:T(8,128)(2,1)S(1)}, bf16[4,704,128]{2,1,0:T(8,128)(2,1)S(1)}, u32[]{:S(2)}, u32[]{:S(2)}) collective-permute-start(bf16[4,704,128]{2,1,0:T(8,128)(2,1)S(1)} %get-tuple-element.263), channel_id=1, source_target_pairs={{0,8},{4,12},{8,0},{12,4},{16,24},{20,28},{24,16},{28,20},{1,9},{5... | collective-permute-start | bytes 2162696 | tf_op jit(solution)/shard_map/ppermute | solution.py:59
  86.9 12.1 %collective-permute-start.16 = (bf16[256,1024]{1,0:T(8,128)(2,1)S(1)}, bf16[256,1024]{1,0:T(8,128)(2,1)S(1)}, u32[]{:S(2)}, u32[]{:S(2)}) collective-permute-start(bf16[256,1024]{1,0:T(8,128)(2,1)S(1)} %get-tuple-element.239), channel_id=1, source_target_pairs={{0,1},{1,0},{2,3},{3,2},{4,5},{5,4},{6,7},{7,6},{8,9},{9,8},{10,11... | collective-permute-start | bytes 1572872 | tf_op jit(solution)/shard_map/ppermute | solution.py:59
  87.0 12.0 %collective-permute-start.19 = (bf16[256,1024]{1,0:T(8,128)(2,1)S(1)}, bf16[256,1024]{1,0:T(8,128)(2,1)S(1)}, u32[]{:S(2)}, u32[]{:S(2)}) collective-permute-start(bf16[256,1024]{1,0:T(8,128)(2,1)S(1)} %get-tuple-element.253), channel_id=1, source_target_pairs={{0,1},{1,0},{2,3},{3,2},{4,5},{5,4},{6,7},{7,6},{8,9},{9,8},{10,11... | collective-permute-start | bytes 1572872 | tf_op jit(solution)/shard_map/ppermute | solution.py:59
  96.9 14.6 %collective-permute-start.21 = (bf16[4,256,128]{2,1,0:T(8,128)(2,1)S(1)}, bf16[4,256,128]{2,1,0:T(8,128)(2,1)S(1)}, u32[]{:S(2)}, u32[]{:S(2)}) collective-permute-start(bf16[4,256,128]{2,1,0:T(8,128)(2,1)S(1)} %get-tuple-element.265), channel_id=1, source_target_pairs={{0,4},{4,0},{8,12},{12,8},{16,20},{20,16},{24,28},{28,24},{1,5},{5... | collective-permute-start | bytes 786440 | tf_op jit(solution)/shard_map/ppermute | solution.py:59
  97.6 16.9 %collective-permute-start.24 = (bf16[256,1024]{1,0:T(8,128)(2,1)S(1)}, bf16[256,1024]{1,0:T(8,128)(2,1)S(1)}, u32[]{:S(2)}, u32[]{:S(2)}) collective-permute-start(bf16[256,1024]{1,0:T(8,128)(2,1)S(1)} %get-tuple-element.268.refs_6_), channel_id=1, source_target_pairs={{0,2},{1,3},{2,0},{3,1},{4,6},{5,7},{6,4},{7,5},{8,10},{9,11},{10,... | collective-permute-start | bytes 1572872 | tf_op jit(solution)/shard_map/ppermute | solution.py:59
  112.2 6.8 %collective-permute-start.23 = (bf16[4,256,128]{2,1,0:T(8,128)(2,1)S(1)}, bf16[4,256,128]{2,1,0:T(8,128)(2,1)S(1)}, u32[]{:S(2)}, u32[]{:S(2)}) collective-permute-start(bf16[4,256,128]{2,1,0:T(8,128)(2,1)S(1)} %back_pair.1.pair), channel_id=1, source_target_pairs={{0,8},{4,12},{8,0},{12,4},{16,24},{20,28},{24,16},{28,20},{1,9},{5... | collective-permute-start | bytes 786440 | tf_op jit(solution)/shard_map/ppermute | solution.py:59
  112.9 26.3 %collective-permute-start.22 = (bf16[4,704,128]{2,1,0:T(8,128)(2,1)S(1)}, bf16[4,704,128]{2,1,0:T(8,128)(2,1)S(1)}, u32[]{:S(2)}, u32[]{:S(2)}) collective-permute-start(bf16[4,704,128]{2,1,0:T(8,128)(2,1)S(1)} %get-tuple-element.266), channel_id=1, source_target_pairs={{0,4},{4,0},{8,12},{12,8},{16,20},{20,16},{24,28},{28,24},{1,5},{5... | collective-permute-start | bytes 2162696 | tf_op jit(solution)/shard_map/ppermute | solution.py:59
  119.7 19.6 %collective-permute-start.27 = (bf16[256,1024]{1,0:T(8,128)(2,1)S(1)}, bf16[256,1024]{1,0:T(8,128)(2,1)S(1)}, u32[]{:S(2)}, u32[]{:S(2)}) collective-permute-start(bf16[256,1024]{1,0:T(8,128)(2,1)S(1)} %collective-permute-done.24.refs_7_), channel_id=1, source_target_pairs={{0,1},{1,0},{2,3},{3,2},{4,5},{5,4},{6,7},{7,6},{8,9},{9,8},{10,11... | collective-permute-start | bytes 1572872 | tf_op jit(solution)/shard_map/ppermute | solution.py:59
  119.8 12.0 %collective-permute-start.25 = (bf16[256,768]{1,0:T(8,128)(2,1)S(1)}, bf16[256,768]{1,0:T(8,128)(2,1)S(1)}, u32[]{:S(2)}, u32[]{:S(2)}) collective-permute-start(bf16[256,768]{1,0:T(8,128)(2,1)S(1)} %get-tuple-element.272), channel_id=1, source_target_pairs={{0,2},{1,3},{2,0},{3,1},{4,6},{5,7},{6,4},{7,5},{8,10},{9,11},{10,... | collective-permute-start | bytes 1179656 | tf_op jit(solution)/shard_map/ppermute | solution.py:59
  120.5 18.8 %collective-permute-start.26 = (bf16[256,768]{1,0:T(8,128)(2,1)S(1)}, bf16[256,768]{1,0:T(8,128)(2,1)S(1)}, u32[]{:S(2)}, u32[]{:S(2)}) collective-permute-start(bf16[256,768]{1,0:T(8,128)(2,1)S(1)} %get-tuple-element.274), channel_id=1, source_target_pairs={{0,3},{1,2},{2,1},{3,0},{4,7},{5,6},{6,5},{7,4},{8,11},{9,10},{10,... | collective-permute-start | bytes 1179656 | tf_op jit(solution)/shard_map/ppermute | solution.py:59
  121.6 17.6 %collective-permute-start.28 = (bf16[4,256,128]{2,1,0:T(8,128)(2,1)S(1)}, bf16[4,256,128]{2,1,0:T(8,128)(2,1)S(1)}, u32[]{:S(2)}, u32[]{:S(2)}) collective-permute-start(bf16[4,256,128]{2,1,0:T(8,128)(2,1)S(1)} %back_quad.1), channel_id=1, source_target_pairs={{0,16},{4,20},{8,24},{12,28},{16,0},{20,4},{24,8},{28,12},{1,17},{... | collective-permute-start | bytes 786440 | tf_op jit(solution)/shard_map/ppermute | solution.py:59
  140.1 6.1 %collective-permute-start.31 = (bf16[256,768]{1,0:T(8,128)(2,1)S(1)}, bf16[256,768]{1,0:T(8,128)(2,1)S(1)}, u32[]{:S(2)}, u32[]{:S(2)}) collective-permute-start(bf16[256,768]{1,0:T(8,128)(2,1)S(1)} %get-tuple-element.286), channel_id=1, source_target_pairs={{0,1},{1,0},{2,3},{3,2},{4,5},{5,4},{6,7},{7,6},{8,9},{9,8},{10,11... | collective-permute-start | bytes 1179656 | tf_op jit(solution)/shard_map/ppermute | solution.py:59
  140.4 8.4 %collective-permute-start.30 = (bf16[4,256,128]{2,1,0:T(8,128)(2,1)S(1)}, bf16[4,256,128]{2,1,0:T(8,128)(2,1)S(1)}, u32[]{:S(2)}, u32[]{:S(2)}) collective-permute-start(bf16[4,256,128]{2,1,0:T(8,128)(2,1)S(1)} %get-tuple-element.277), channel_id=1, source_target_pairs={{0,4},{4,0},{8,12},{12,8},{16,20},{20,16},{24,28},{28,24},{1,5},{5... | collective-permute-start | bytes 786440 | tf_op jit(solution)/shard_map/ppermute | solution.py:59
  142.6 10.7 %collective-permute-start.33 = (bf16[2,704,128]{2,1,0:T(8,128)(2,1)S(1)}, bf16[2,704,128]{2,1,0:T(8,128)(2,1)S(1)}, u32[]{:S(2)}, u32[]{:S(2)}) collective-permute-start(bf16[2,704,128]{2,1,0:T(8,128)(2,1)S(1)} %get-tuple-element.302), channel_id=1, source_target_pairs={{0,8},{4,12},{8,0},{12,4},{16,24},{20,28},{24,16},{28,20},{1,9},{5... | collective-permute-start | bytes 1081352 | tf_op jit(solution)/shard_map/ppermute | solution.py:59
  150.6 30.6 %collective-permute-start.37 = (bf16[4,128,768]{2,1,0:T(8,128)(2,1)S(1)}, bf16[4,128,768]{2,1,0:T(8,128)(2,1)S(1)}, u32[]{:S(2)}, u32[]{:S(2)}) collective-permute-start(bf16[4,128,768]{2,1,0:T(8,128)(2,1)S(1)} %get-tuple-element.317), channel_id=1, source_target_pairs={{0,4},{4,0},{8,12},{12,8},{16,20},{20,16},{24,28},{28,24},{1,5},{5... | collective-permute-start | bytes 2359304 | tf_op jit(solution)/shard_map/ppermute | solution.py:59
  152.1 9.1 %collective-permute-start.34 = (bf16[256,512]{1,0:T(8,128)(2,1)S(1)}, bf16[256,512]{1,0:T(8,128)(2,1)S(1)}, u32[]{:S(2)}, u32[]{:S(2)}) collective-permute-start(bf16[256,512]{1,0:T(8,128)(2,1)S(1)} %get-tuple-element.308), channel_id=1, source_target_pairs={{0,2},{1,3},{2,0},{3,1},{4,6},{5,7},{6,4},{7,5},{8,10},{9,11},{10,... | collective-permute-start | bytes 786440 | tf_op jit(solution)/shard_map/ppermute | solution.py:59
  152.7 15.2 %collective-permute-start.29 = (bf16[2,704,128]{2,1,0:T(8,128)(2,1)S(1)}, bf16[2,704,128]{2,1,0:T(8,128)(2,1)S(1)}, u32[]{:S(2)}, u32[]{:S(2)}) collective-permute-start(bf16[2,704,128]{2,1,0:T(8,128)(2,1)S(1)} %get-tuple-element.284), channel_id=1, source_target_pairs={{0,8},{4,12},{8,0},{12,4},{16,24},{20,28},{24,16},{28,20},{1,9},{5... | collective-permute-start | bytes 1081352 | tf_op jit(solution)/shard_map/ppermute | solution.py:59
  153.4 12.7 %collective-permute-start.35 = (bf16[256,512]{1,0:T(8,128)(2,1)S(1)}, bf16[256,512]{1,0:T(8,128)(2,1)S(1)}, u32[]{:S(2)}, u32[]{:S(2)}) collective-permute-start(bf16[256,512]{1,0:T(8,128)(2,1)S(1)} %get-tuple-element.310), channel_id=1, source_target_pairs={{0,3},{1,2},{2,1},{3,0},{4,7},{5,6},{6,5},{7,4},{8,11},{9,10},{10,... | collective-permute-start | bytes 786440 | tf_op jit(solution)/shard_map/ppermute | solution.py:59
  154.4 24.4 %collective-permute-start.39 = (bf16[2,704,128]{2,1,0:T(8,128)(2,1)S(1)}, bf16[2,704,128]{2,1,0:T(8,128)(2,1)S(1)}, u32[]{:S(2)}, u32[]{:S(2)}) collective-permute-start(bf16[2,704,128]{2,1,0:T(8,128)(2,1)S(1)} %get-tuple-element.319), channel_id=1, source_target_pairs={{0,4},{4,0},{8,12},{12,8},{16,20},{20,16},{24,28},{28,24},{1,5},{5... | collective-permute-start | bytes 1081352 | tf_op jit(solution)/shard_map/ppermute | solution.py:59
  161.2 10.6 %collective-permute-start.40 = (bf16[1,704,128]{2,1,0:T(8,128)(2,1)S(1)}, bf16[1,704,128]{2,1,0:T(8,128)(2,1)S(1)}, u32[]{:S(2)}, u32[]{:S(2)}) collective-permute-start(bf16[1,704,128]{2,1,0:T(8,128)(2,1)S(1)} %get-tuple-element.320), channel_id=1, source_target_pairs={{0,16},{4,20},{8,24},{12,28},{16,0},{20,4},{24,8},{28,12},{1,17},{... | collective-permute-start | bytes 540680 | tf_op jit(solution)/shard_map/ppermute | solution.py:59
  168.6 11.8 %collective-permute-start.38 = (bf16[1,704,128]{2,1,0:T(8,128)(2,1)S(1)}, bf16[1,704,128]{2,1,0:T(8,128)(2,1)S(1)}, u32[]{:S(2)}, u32[]{:S(2)}) collective-permute-start(bf16[1,704,128]{2,1,0:T(8,128)(2,1)S(1)} %get-tuple-element.318), channel_id=1, source_target_pairs={{0,16},{4,20},{8,24},{12,28},{16,0},{20,4},{24,8},{28,12},{1,17},{... | collective-permute-start | bytes 540680 | tf_op jit(solution)/shard_map/ppermute | solution.py:59
  171.0 26.2 %collective-permute-start.36 = (bf16[256,1024]{1,0:T(8,128)(2,1)S(1)}, bf16[256,1024]{1,0:T(8,128)(2,1)S(1)}, u32[]{:S(2)}, u32[]{:S(2)}) collective-permute-start(bf16[256,1024]{1,0:T(8,128)(2,1)S(1)} %down_add.1), channel_id=1, source_target_pairs={{0,2},{1,3},{2,0},{3,1},{4,6},{5,7},{6,4},{7,5},{8,10},{9,11},{10,... | collective-permute-start | bytes 1572872 | tf_op jit(solution)/shard_map/ppermute | solution.py:59
  171.8 27.8 %collective-permute-start.42 = (bf16[4,128,512]{2,1,0:T(8,128)(2,1)S(1)}, bf16[4,128,512]{2,1,0:T(8,128)(2,1)S(1)}, u32[]{:S(2)}, u32[]{:S(2)}) collective-permute-start(bf16[4,128,512]{2,1,0:T(8,128)(2,1)S(1)} %get-tuple-element.338), channel_id=1, source_target_pairs={{0,4},{4,0},{8,12},{12,8},{16,20},{20,16},{24,28},{28,24},{1,5},{5... | collective-permute-start | bytes 1572872 | tf_op jit(solution)/shard_map/ppermute | solution.py:59
  181.9 14.7 %collective-permute-start.41 = (bf16[2,128,768]{2,1,0:T(8,128)(2,1)S(1)}, bf16[2,128,768]{2,1,0:T(8,128)(2,1)S(1)}, u32[]{:S(2)}, u32[]{:S(2)}) collective-permute-start(bf16[2,128,768]{2,1,0:T(8,128)(2,1)S(1)} %get-tuple-element.331), channel_id=1, source_target_pairs={{0,8},{4,12},{8,0},{12,4},{16,24},{20,28},{24,16},{28,20},{1,9},{5... | collective-permute-start | bytes 1179656 | tf_op jit(solution)/shard_map/ppermute | solution.py:59
  182.4 16.4 %collective-permute-start.43 = (bf16[1,704,128]{2,1,0:T(8,128)(2,1)S(1)}, bf16[1,704,128]{2,1,0:T(8,128)(2,1)S(1)}, u32[]{:S(2)}, u32[]{:S(2)}) collective-permute-start(bf16[1,704,128]{2,1,0:T(8,128)(2,1)S(1)} %get-tuple-element.339), channel_id=1, source_target_pairs={{0,16},{4,20},{8,24},{12,28},{16,0},{20,4},{24,8},{28,12},{1,17},{... | collective-permute-start | bytes 540680 | tf_op jit(solution)/shard_map/ppermute | solution.py:59
  200.2 11.3 %collective-permute-start.44 = (bf16[2,128,512]{2,1,0:T(8,128)(2,1)S(1)}, bf16[2,128,512]{2,1,0:T(8,128)(2,1)S(1)}, u32[]{:S(2)}, u32[]{:S(2)}) collective-permute-start(bf16[2,128,512]{2,1,0:T(8,128)(2,1)S(1)} %get-tuple-element.345), channel_id=1, source_target_pairs={{0,8},{4,12},{8,0},{12,4},{16,24},{20,28},{24,16},{28,20},{1,9},{5... | collective-permute-start | bytes 786440 | tf_op jit(solution)/shard_map/ppermute | solution.py:59
  200.4 9.0 %collective-permute-start.45 = (bf16[1,128,768]{2,1,0:T(8,128)(2,1)S(1)}, bf16[1,128,768]{2,1,0:T(8,128)(2,1)S(1)}, u32[]{:S(2)}, u32[]{:S(2)}) collective-permute-start(bf16[1,128,768]{2,1,0:T(8,128)(2,1)S(1)} %get-tuple-element.346), channel_id=1, source_target_pairs={{0,16},{4,20},{8,24},{12,28},{16,0},{20,4},{24,8},{28,12},{1,17},{... | collective-permute-start | bytes 589832 | tf_op jit(solution)/shard_map/ppermute | solution.py:59
  212.2 8.6 %collective-permute-start.46 = (bf16[1,128,512]{2,1,0:T(8,128)(2,1)S(1)}, bf16[1,128,512]{2,1,0:T(8,128)(2,1)S(1)}, u32[]{:S(2)}, u32[]{:S(2)}) collective-permute-start(bf16[1,128,512]{2,1,0:T(8,128)(2,1)S(1)} %get-tuple-element.352), channel_id=1, source_target_pairs={{0,16},{4,20},{8,24},{12,28},{16,0},{20,4},{24,8},{28,12},{1,17},{... | collective-permute-start | bytes 393224 | tf_op jit(solution)/shard_map/ppermute | solution.py:59
  214.3 7.1 %collective-permute-start.50 = (bf16[128,768]{1,0:T(8,128)(2,1)S(1)}, bf16[128,768]{1,0:T(8,128)(2,1)S(1)}, u32[]{:S(2)}, u32[]{:S(2)}) collective-permute-start(bf16[128,768]{1,0:T(8,128)(2,1)S(1)} %d_early_sum.1.refs_1_), channel_id=1, source_target_pairs={{0,2},{1,3},{2,0},{3,1},{4,6},{5,7},{6,4},{7,5},{8,10},{9,11},{10,... | collective-permute-start | bytes 589832 | tf_op jit(solution)/shard_map/ppermute | solution.py:59
  220.9 5.0 %collective-permute-start.47 = (bf16[128,512]{1,0:T(8,128)(2,1)S(1)}, bf16[128,512]{1,0:T(8,128)(2,1)S(1)}, u32[]{:S(2)}, u32[]{:S(2)}) collective-permute-start(bf16[128,512]{1,0:T(8,128)(2,1)S(1)} %d_late_sum.1.refs_5_), channel_id=1, source_target_pairs={{0,2},{1,3},{2,0},{3,1},{4,6},{5,7},{6,4},{7,5},{8,10},{9,11},{10,... | collective-permute-start | bytes 393224 | tf_op jit(solution)/shard_map/ppermute | solution.py:59
  221.5 5.8 %collective-permute-start.49 = (bf16[128,768]{1,0:T(8,128)(2,1)S(1)}, bf16[128,768]{1,0:T(8,128)(2,1)S(1)}, u32[]{:S(2)}, u32[]{:S(2)}) collective-permute-start(bf16[128,768]{1,0:T(8,128)(2,1)S(1)} %d_early_sum.1.refs_1_), channel_id=1, source_target_pairs={{0,1},{1,0},{2,3},{3,2},{4,5},{5,4},{6,7},{7,6},{8,9},{9,8},{10,11... | collective-permute-start | bytes 589832 | tf_op jit(solution)/shard_map/ppermute | solution.py:59
  221.5 6.0 %collective-permute-start.51 = (bf16[128,768]{1,0:T(8,128)(2,1)S(1)}, bf16[128,768]{1,0:T(8,128)(2,1)S(1)}, u32[]{:S(2)}, u32[]{:S(2)}) collective-permute-start(bf16[128,768]{1,0:T(8,128)(2,1)S(1)} %collective-permute-done.50.refs_3_), channel_id=1, source_target_pairs={{0,1},{1,0},{2,3},{3,2},{4,5},{5,4},{6,7},{7,6},{8,9},{9,8},{10,11... | collective-permute-start | bytes 589832 | tf_op jit(solution)/shard_map/ppermute | solution.py:59
  (17 other events, 123.2 us)
